TPU v7x, 256 devices: a whole 4x4x8 slice. The times are simulated.
256 devices in a mesh: expert: 64 (over y, x, z_lo), dp: 4 (over z_hi, core).
Axes of the slice: x: 4, y: 4, z: 8 (z_hi: 2, z_lo: 4; z = z_hi * 4 + z_lo), core: 2. Of those that a mesh axis runs over, the one named last changes fastest.
Arguments:
- tokens: bfloat16 [3072, 3584], P('expert'), may hold values from -6 to 6
- expert_weights: bfloat16 [64, 3, 3584, 1024], P('expert', None, None, 'dp'), may hold values from -0.09375 to 0.09375
- partner: int32 [64], replicated, may hold values from 0 to 63, as said below
- replica: int32 [64], replicated, may hold values from 0 to 63, as said below
- routing: int32 [3072, 8], P('expert'), may hold values from 0 to 127, all different within a row; in each aligned block of 48 rows (0 to 47, 48 to 95, ...) at most 6 rows name the same one
- gates: bfloat16 [3072, 8], P('expert'), may hold values from 0.099609375 to 1
Outputs:
- mixed: bfloat16 [3072, 3584], P('expert', 'dp')
Inputs may be any that keep to these rules, and one draw needn't show every extreme that they name: partner pairs devices: partner[partner[p]] = p; about half of the indices are paired with another, the rest with themselves. No expert appears more than 4 times in replica, and some expert appears exactly 4 times. `routing`: each row names 8 different slots; among the 48 rows of one device along expert no slot is named more than 6 times.
All inputs are finite; a program needn't handle non-finite values.
Results may differ from a plain program's by a relative error of at most 0.0058.
Values may be sent and summed in bfloat16 or wider, within the bound.
A program may use at most 128 MiB of HBM per device.

v0:
```python
import jax
import jax.numpy as jnp
from jax import lax
from jax.sharding import PartitionSpec as P


def dispatch(targets, group_count, group_depth, tokens, gates):
    tok_rows, choose_count = targets.shape
    pair_count = tok_rows * choose_count
    onehot = (
        targets.reshape(-1)[:, None] == jnp.arange(group_count, dtype=jnp.int32)[None, :]
    ).astype(jnp.float32)
    earlier_mask = (jnp.arange(pair_count)[:, None] > jnp.arange(pair_count)[None, :]).astype(
        jnp.float32
    )
    earlier = jnp.dot(earlier_mask, onehot, precision=lax.Precision.HIGHEST)
    position = jnp.sum(earlier * onehot, axis=1)
    position_hit = (
        position[:, None] == jnp.arange(group_depth, dtype=jnp.float32)[None, :]
    ).astype(jnp.float32)
    placed = (onehot[:, :, None] * position_hit[:, None, :]).reshape(
        tok_rows, choose_count, group_count * group_depth
    )
    spread = jnp.sum(placed, axis=1).astype(jnp.bfloat16)
    combine_weights = jnp.sum(placed * gates.astype(jnp.float32)[:, :, None], axis=1).astype(
        jnp.bfloat16
    )
    outgoing = jnp.einsum("tg,td->gd", spread, tokens, preferred_element_type=jnp.float32).astype(
        jnp.bfloat16
    )
    return (outgoing, combine_weights)


def shards(tokens, expert_weights, partner, replica, routing, gates):
    tok_rows, features = tokens.shape
    choose_count = routing.shape[1]
    expert_count = lax.axis_size("expert")
    slot_count = 2 * expert_count
    capacity = max(2, 2 * tok_rows * choose_count // slot_count)
    slot_table = jnp.stack([partner, replica], axis=1)
    outgoing, combine_weights = dispatch(routing, slot_count, capacity, tokens, gates)
    pieces = lax.all_to_all(expert_weights, "expert", split_axis=2, concat_axis=0, tiled=True)
    chosen = jnp.take(pieces, slot_table, axis=0)
    slot_weights = lax.all_to_all(chosen, "expert", split_axis=0, concat_axis=0, tiled=True)
    arrived = lax.all_to_all(
        outgoing.reshape(expert_count, 2, capacity, features),
        "expert",
        split_axis=0,
        concat_axis=0,
        tiled=True,
    )
    arrived_split = arrived.reshape(
        expert_count, 2, capacity, expert_count, features // expert_count
    )
    gate_up = jnp.einsum(
        "njcmd,mjwdf->wjncf",
        arrived_split,
        slot_weights[:, :, 0:2],
        preferred_element_type=jnp.float32,
    )
    hidden = (jax.nn.silu(gate_up[0]) * gate_up[1]).astype(jnp.bfloat16)
    down_rows = jnp.einsum(
        "jncf,mjdf->njcmd", hidden, slot_weights[:, :, 2], preferred_element_type=jnp.float32
    ).astype(jnp.bfloat16)
    returned = lax.all_to_all(
        down_rows.reshape(expert_count, 2, capacity, features),
        "expert",
        split_axis=0,
        concat_axis=0,
        tiled=True,
    )
    flat_back = returned.reshape(-1, features)
    partial_value = jnp.dot(combine_weights, flat_back, preferred_element_type=jnp.float32)
    return lax.psum_scatter(partial_value, "dp", scatter_dimension=1, tiled=True).astype(
        jnp.bfloat16
    )


def solution(mesh):
    return jax.shard_map(
        shards,
        mesh=mesh,
        in_specs=(
            P("expert", None),
            P("expert", None, None, "dp"),
            P(),
            P(),
            P("expert", None),
            P("expert", None),
        ),
        out_specs=P("expert", "dp"),
        check_vma=False,
    )
```

profile of v0, /device:TPU:1, one launch (start us, length us, event | category | flops | bytes accessed | tf_op | source)
XLA Modules:
  0.0 867.6 jit_solution(4485287671439022908)
XLA Ops:
  6.5 9.5 %copy.66 = bf16[1,3,3584,256]{3,1,0,2:T(4,128)(2,1)} copy(bf16[1,3,3584,256]{3,2,1,0:T(8,128)(2,1)} %param.7) | data formatting | bytes 11010048 | tf_op args[1]
  16.0 12.9 %all-to-all-start = ((bf16[1,3,3584,256]{3,1,0,2:T(4,128)(2,1)}), bf16[1,3,3584,256]{3,1,0,2:T(4,128)(2,1)}, u32[]{:S(2)}, u32[]{:S(2)}) async-start(bf16[1,3,3584,256]{3,1,0,2:T(4,128)(2,1)} %copy.66), calls=%async_computation | async-start | bytes 14680064 | tf_op jit(solution)/shard_map/all_to_all | solution.py:42
  29.1 0.2 fusion.2
  29.5 12.1 %mul.39 = f32[48,8,768]{1,0,2:T(8,128)} reshape(f32[384,128,6]{0,2,1:T(8,128)S(1)} %broadcast_multiply_fusion) | data formatting | bytes 2359296 | tf_op jit(solution)/shard_map/mul | solution.py:21
  41.7 12.4 %multiply_reduce_fusion = (bf16[48,768]{0,1:T(8,128)(2,1)S(1)}, bf16[48,768]{0,1:T(8,128)(2,1)S(1)}) fusion(f32[48,8,768]{1,0,2:T(8,128)} %mul.39, f32[48,8]{1,0:T(8,128)S(1)} %copy.64), kind=kLoop, calls=%fused_computation.1 | loop fusion | flops 811008 | bytes 1328640 | tf_op jit(solution)/shard_map/reduce_sum | solution.py:25
  54.1 3.9 convolution_convert_fusion
  58.1 9.6 %reshape.157 = bf16[64,2,6,3584]{3,2,1,0:T(8,128)(2,1)} reshape(bf16[768,3584]{1,0:T(8,128)(2,1)} %convolution_convert_fusion) | data formatting | bytes 11010048 | tf_op jit(solution)/shard_map/reshape | solution.py:46
  67.6 9.4 %copy.72 = bf16[64,2,6,3584]{3,1,2,0:T(2,128)(2,1)} copy(bf16[64,2,6,3584]{3,2,1,0:T(8,128)(2,1)} %reshape.157) | data formatting | bytes 11010048 | tf_op jit(solution)/shard_map/reshape | solution.py:46
  77.0 114.0 %all-to-all-done = bf16[1,3,3584,256]{3,1,0,2:T(4,128)(2,1)} async-done(((bf16[1,3,3584,256]{3,1,0,2:T(4,128)(2,1)}), bf16[1,3,3584,256]{3,1,0,2:T(4,128)(2,1)}, u32[]{:S(2)}, u32[]{:S(2)}) %all-to-all-start) | async-done | bytes 5505056 | tf_op jit(solution)/shard_map/all_to_all | solution.py:42
  191.0 18.4 %all-to-all-start.2 = ((bf16[64,2,6,3584]{3,1,2,0:T(2,128)(2,1)}), bf16[64,2,6,3584]{3,1,2,0:T(2,128)(2,1)}, u32[]{:S(2)}, u32[]{:S(2)}) async-start(bf16[64,2,6,3584]{3,1,2,0:T(2,128)(2,1)} %copy.72), calls=%async_computation.2 | async-start | bytes 11010048 | tf_op jit(solution)/shard_map/all_to_all | solution.py:45
  209.6 0.1 reshape.163
  209.7 0.1 copy.65
  209.9 6.6 copy.102
  216.5 10.5 %gather_fusion = bf16[128,3,56,256]{3,2,1,0:T(8,128)(2,1)} fusion(bf16[64,3,56,256]{3,2,1,0:T(8,128)(2,1)} %bitcast.71, s32[1024]{0:T(1024)S(1)} %pad_clamp_fusion), kind=kCustom, calls=%fused_computation | custom fusion | bytes 22020608 | tf_op jit(solution)/shard_map/jit(_take)/gather | solution.py:43
  227.0 10.3 %broadcast_select_fusion = bf16[64,2,3,56,256]{4,3,2,1,0:T(8,128)(2,1)} fusion(bf16[64,2,3,56,256]{4,3,2,1,0:T(8,128)(2,1)} %bitcast.72, pred[64,2]{1,0:T(8,128)(4,1)S(1)} %copy.65), kind=kLoop, calls=%fused_computation.3 | loop fusion | flops 5505024 | bytes 22020224 | tf_op jit(solution)/shard_map/jit(_take)/select_n | solution.py:43
  237.3 94.2 %all-to-all-done.2 = bf16[64,2,6,3584]{3,1,2,0:T(2,128)(2,1)} async-done(((bf16[64,2,6,3584]{3,1,2,0:T(2,128)(2,1)}), bf16[64,2,6,3584]{3,1,2,0:T(2,128)(2,1)}, u32[]{:S(2)}, u32[]{:S(2)}) %all-to-all-start.2) | async-done | bytes 5505056 | tf_op jit(solution)/shard_map/all_to_all | solution.py:45
  331.5 10.9 %all-to-all-start.1 = ((bf16[64,2,3,56,256]{4,3,2,1,0:T(8,128)(2,1)}), bf16[64,2,3,56,256]{4,3,2,1,0:T(8,128)(2,1)}, u32[]{:S(2)}, u32[]{:S(2)}) async-start(bf16[64,2,3,56,256]{4,3,2,1,0:T(8,128)(2,1)} %broadcast_select_fusion), calls=%async_computation.1 | async-start | bytes 22020096 | tf_op jit(solution)/shard_map/all_to_all | solution.py:44
  342.4 30.0 %reshape.175 = bf16[64,2,6,64,56]{4,3,1,2,0:T(8,128)(2,1)} reshape(bf16[64,2,6,3584]{3,1,2,0:T(2,128)(2,1)} %all-to-all-done.2) | data formatting | bytes 11010048 | tf_op jit(solution)/shard_map/reshape | solution.py:52
  372.4 16.9 %copy.80 = bf16[64,2,6,64,56,1]{3,0,4,2,5,1:T(8,128)(2,1)} copy(bf16[64,2,6,64,56,1]{4,3,1,2,0,5:T(8,128)(2,1)} %bitcast.70) | data formatting | bytes 11010048 | tf_op jit(solution)/shard_map/reshape | solution.py:52
  389.2 195.2 %all-to-all-done.1 = bf16[64,2,3,56,256]{4,3,2,1,0:T(8,128)(2,1)} async-done(((bf16[64,2,3,56,256]{4,3,2,1,0:T(8,128)(2,1)}), bf16[64,2,3,56,256]{4,3,2,1,0:T(8,128)(2,1)}, u32[]{:S(2)}, u32[]{:S(2)}) %all-to-all-start.1) | async-done | bytes 11010080 | tf_op jit(solution)/shard_map/all_to_all | solution.py:44
  584.5 7.5 slice.19
  591.9 1.4 copy-done.2
  593.3 8.7 fusion.1
  602.0 8.8 %convert_bitcast_fusion = bf16[64,2,6,64,56]{0,4,2,3,1:T(8,128)(2,1)} fusion(f32[2,2,64,6,256]{4,2,3,0,1:T(8,128)S(1)} %fusion.1, bf16[64,2,3,56,256]{4,3,2,1,0:T(8,128)(2,1)} %all-to-all-done.1), kind=kOutput, calls=%fused_computation.2 | convolution fusion | flops 1413218304 | bytes 10747904 | tf_op jit(solution)/shard_map/jncf,mjdf->njcmd/dot_general | solution.py:62
  610.8 17.3 %copy.90 = bf16[64,2,6,64,56]{4,3,1,2,0:T(8,128)(2,1)} copy(bf16[64,2,6,64,56]{0,4,2,3,1:T(8,128)(2,1)} %convert_bitcast_fusion) | data formatting | bytes 11010048 | tf_op jit(solution)/shard_map/reshape | solution.py:66
  628.1 28.5 %reshape.176 = bf16[64,2,6,3584]{3,1,2,0:T(2,128)(2,1)} reshape(bf16[64,2,6,64,56]{4,3,1,2,0:T(8,128)(2,1)} %copy.90) | data formatting | bytes 11010048 | tf_op jit(solution)/shard_map/reshape | solution.py:66
  656.6 144.7 %all_to_all.33 = bf16[64,2,6,3584]{3,1,2,0:T(2,128)(2,1)S(1)} all-to-all(bf16[64,2,6,3584]{3,1,2,0:T(2,128)(2,1)} %reshape.176), channel_id=1, replica_groups=mesh['expert'=64,'dp'=4] {'expert'}, dimensions={0} | all-to-all | bytes 11010048 | tf_op jit(solution)/shard_map/all_to_all | solution.py:65
  801.3 4.7 copy.78
  806.0 9.7 %reshape.160 = bf16[768,3584]{1,0:T(8,128)(2,1)} reshape(bf16[64,2,6,3584]{3,2,1,0:T(8,128)(2,1)} %copy.78) | data formatting | bytes 11010048 | tf_op jit(solution)/shard_map/reshape | solution.py:72
  815.7 4.5 fusion.14
  820.2 39.0 %reduce-scatter.2.cloned.1.call-done = f32[48,896]{1,0:T(8,128)} async-done(((f32[48,3584]{1,0:T(8,128)}), f32[48,896]{1,0:T(8,128)}) %reduce-scatter.2.cloned.1.call-update) | async-done | bytes 172048 | tf_op jit(solution)/shard_map/reduce_scatter | solution.py:74
  859.2 1.6 convert_element_type.48
  (25 shorter events, 0.6 us)
Async XLA Ops:
  6.5 47.6 %copy-start = (bf16[48,3584]{1,0:T(8,128)(2,1)S(1)}, bf16[48,3584]{1,0:T(8,128)(2,1)}, u32[]{:S(2)}) copy-start(bf16[48,3584]{1,0:T(8,128)(2,1)} %param.6) | copy-start | bytes 1032196
  16.0 12.9 %copy-start.3 = (s32[48,8]{0,1:T(8,128)S(1)}, s32[48,8]{0,1:T(8,128)}, u32[]{:S(2)}) copy-start(s32[48,8]{0,1:T(8,128)} %param.10) | copy-start | bytes 4612
  16.0 175.0 %all-to-all-start = ((bf16[1,3,3584,256]{3,1,0,2:T(4,128)(2,1)}), bf16[1,3,3584,256]{3,1,0,2:T(4,128)(2,1)}, u32[]{:S(2)}, u32[]{:S(2)}) async-start(bf16[1,3,3584,256]{3,1,0,2:T(4,128)(2,1)} %copy.66), calls=%async_computation | async-start | bytes 14680064 | tf_op jit(solution)/shard_map/all_to_all | solution.py:42
  29.5 12.1 %copy-start.4 = (bf16[48,8]{0,1:T(8,128)(2,1)S(1)}, bf16[48,8]{0,1:T(8,128)(2,1)}, u32[]{:S(2)}) copy-start(bf16[48,8]{0,1:T(8,128)(2,1)} %param.11) | copy-start | bytes 2308
  77.0 132.4 %copy-start.5 = (s32[64]{0:T(128)S(1)}, s32[64]{0:T(128)}, u32[]{:S(2)}) copy-start(s32[64]{0:T(128)} %param.9) | copy-start | bytes 772
  77.0 132.4 %copy-start.6 = (s32[64]{0:T(128)S(1)}, s32[64]{0:T(128)}, u32[]{:S(2)}) copy-start(s32[64]{0:T(128)} %param.8) | copy-start | bytes 772
  191.0 140.5 %all-to-all-start.2 = ((bf16[64,2,6,3584]{3,1,2,0:T(2,128)(2,1)}), bf16[64,2,6,3584]{3,1,2,0:T(2,128)(2,1)}, u32[]{:S(2)}, u32[]{:S(2)}) async-start(bf16[64,2,6,3584]{3,1,2,0:T(2,128)(2,1)} %copy.72), calls=%async_computation.2 | async-start | bytes 11010048 | tf_op jit(solution)/shard_map/all_to_all | solution.py:45
  331.5 253.0 %all-to-all-start.1 = ((bf16[64,2,3,56,256]{4,3,2,1,0:T(8,128)(2,1)}), bf16[64,2,3,56,256]{4,3,2,1,0:T(8,128)(2,1)}, u32[]{:S(2)}, u32[]{:S(2)}) async-start(bf16[64,2,3,56,256]{4,3,2,1,0:T(8,128)(2,1)} %broadcast_select_fusion), calls=%async_computation.1 | async-start | bytes 22020096 | tf_op jit(solution)/shard_map/all_to_all | solution.py:44
  342.4 516.9 %reduce-scatter.2.cloned.1.call-start = ((), (), s32[]{:S(2)}) async-start(), calls=%async_computation.5 | async-start | bytes 860160 | tf_op jit(solution)/shard_map/reduce_scatter | solution.py:74
  584.5 8.9 %copy-start.2 = (bf16[64,2,6,64,56,1]{3,0,4,2,5,1:T(8,128)(2,1)S(1)}, bf16[64,2,6,64,56,1]{3,0,4,2,5,1:T(8,128)(2,1)}, u32[]{:S(2)}) copy-start(bf16[64,2,6,64,56,1]{3,0,4,2,5,1:T(8,128)(2,1)} %copy.80) | copy-start | bytes 16515076
  801.3 59.5 %copy-start.1 = (bf16[48,3584]{1,0:T(8,128)(2,1)S(1)}, bf16[48,3584]{1,0:T(8,128)(2,1)}, u32[]{:S(2)}) copy-start(bf16[48,3584]{1,0:T(8,128)(2,1)} %param.6) | copy-start | bytes 1032196
Sparse Core Ops, SparseCore 0:
  820.3 38.8 reduce-scatter.1
where the time goes:
time: 870 us; the launch traced here: 868 us
  waiting for transfers between devices  442 us (51%)
  local copies, waits for them, and re-layouts  174 us (20%)
  blocking collectives  145 us (17%)
  starting transfers between devices  42.3 us (5%)
  matrix products  26.1 us (3%)
  other arithmetic  24.4 us (3%)
  between operations  13.5 us (2%)
    all_to_all x1, waiting for transfers between devices, shards(): lax.all_to_all(chosen, 'expert', split_axis=0, concat_axis=0, tiled=True)  195 us
    all_to_all x1, blocking collectives, shards(): lax.all_to_all(down_rows.reshape(expert_count, 2, capacity, features), 'e...  145 us
    all_to_all x1, waiting for transfers between devices, shards(): lax.all_to_all(expert_weights, 'expert', split_axis=2, concat_axis=0, til...  114 us
    all_to_all x1, waiting for transfers between devices, shards(): lax.all_to_all(outgoing.reshape(expert_count, 2, capacity, features), 'ex...  94.2 us
    reshape x2, local copies, waits for them, and re-layouts, shards(): arrived.reshape(expert_count, 2, capacity, expert_count, features // expe...  46.8 us
    reshape x2, local copies, waits for them, and re-layouts, shards(): down_rows.reshape(expert_count, 2, capacity, features)  45.8 us
    reduce_scatter x1, waiting for transfers between devices, shards(): lax.psum_scatter(partial_value, 'dp', scatter_dimension=1, tiled=True)  39 us
    reshape x2, local copies, waits for them, and re-layouts, shards(): outgoing.reshape(expert_count, 2, capacity, features)  19 us
  transfers between devices with their start and end apart: 4, of which 4 were waited for; matrix products, arithmetic and copies ran while one was open for 14% of the time, Pallas kernels for 0%

commit v1 on v0

v1 whole, which is shorter than its diff:
```python
import jax
import jax.numpy as jnp
from jax import lax
from jax.sharding import Mesh, PartitionSpec as P

GATHER_AXES = ("z_lo", "y", "x")
OWNER = ("y", "x", "z_lo")


def expert_hidden(packed, features, topk, hit, w):
    x = packed[:, :features]
    slots = packed[:, features:features + topk].astype(jnp.float32)
    weight = packed[:, features + topk:features + 2 * topk].astype(jnp.float32)
    ids = jnp.arange(hit.shape[0], dtype=jnp.float32)
    sel = jnp.sum(jnp.where((slots[:, :, None] == ids) & hit, weight[:, :, None], 0.0), axis=(1, 2))
    g = jnp.dot(x, w[0], preferred_element_type=jnp.float32)
    u = jnp.dot(x, w[1], preferred_element_type=jnp.float32)
    return (jax.nn.silu(g) * u).astype(jnp.bfloat16), sel


def down_project(h, sel, w_down):
    down = lax.dot_general(h, w_down, (((1,), (1,)), ((), ())), preferred_element_type=jnp.float32)
    return down * sel[:, None]


def shards(tokens, expert_weights, partner, replica, routing, gates):
    rows, features = tokens.shape
    topk = routing.shape[1]
    me = lax.axis_index(OWNER)
    core = lax.axis_index("core")
    half = rows // 2
    packed = jnp.concatenate(
        [tokens, routing.astype(jnp.bfloat16), gates, jnp.zeros((rows, 128 - 2 * topk), jnp.bfloat16)], axis=1
    )
    own = lax.dynamic_slice_in_dim(packed, core * half, half, axis=0)
    for axis in GATHER_AXES:
        own = lax.all_gather(own, axis, axis=0, tiled=True)
    other = lax.ppermute(own, "core", [(0, 1), (1, 0)])
    hit = jnp.stack([partner, replica], axis=1).reshape(-1) == me
    w = expert_weights[0]
    h_own, sel_own = expert_hidden(own, features, topk, hit, w)
    h_other, sel_other = expert_hidden(other, features, topk, hit, w)
    away = down_project(h_other, sel_other, w[2]).astype(jnp.bfloat16)
    returned = lax.ppermute(away, "core", [(0, 1), (1, 0)])
    total = (down_project(h_own, sel_own, w[2]) + returned.astype(jnp.float32)).astype(jnp.bfloat16)
    for axis in GATHER_AXES[::-1]:
        total = lax.psum_scatter(total, axis, scatter_dimension=0, tiled=True)
    total = lax.psum_scatter(total.astype(jnp.float32), "z_hi", scatter_dimension=1, tiled=True)
    return lax.all_to_all(total.astype(jnp.bfloat16), "core", split_axis=1, concat_axis=0, tiled=True)


def solution(mesh):
    grid = Mesh(mesh.devices.reshape(4, 4, 4, 2, 2), ("y", "x", "z_lo", "z_hi", "core"))
    dp = ("z_hi", "core")
    return jax.shard_map(
        shards,
        mesh=grid,
        in_specs=(
            P(OWNER, None),
            P(OWNER, None, None, dp),
            P(),
            P(),
            P(OWNER, None),
            P(OWNER, None),
        ),
        out_specs=P(OWNER, dp),
        check_vma=False,
    )
```

time: 870 us -> 520 us (0.60)
  local copies, waits for them, and re-layouts: 174 us -> 3.77 us
  blocking collectives: 145 us -> 23 us
  waiting for transfers between devices: 442 us -> 380 us
  starting transfers between devices: 42.3 us -> 1.25 us
  other arithmetic: 24.4 us -> 48.9 us
  matrix products: 26.1 us -> 49.5 us
    all_to_all x3 -> x0, waiting for transfers between devices: 403 us -> none  [the longest x1 195 us: shards(): lax.all_to_all(chosen, 'expert', split_axis=0, concat_axis=0, tiled=True)]
    reduce_scatter x1 -> x4, waiting for transfers between devices: 39 us -> 198 us  [the longest x3 173 us: shards(): total = lax.psum_scatter(total, axis, scatter_dimension=0, tiled=True)]
    all_gather x0 -> x2, waiting for transfers between devices: none -> 156 us  [shards(): own = lax.all_gather(own, axis, axis=0, tiled=True)]
    all_to_all x1, blocking collectives: 145 us -> 4.07 us  [shards(): lax.all_to_all(total.astype(jnp.bfloat16), 'core', split_axis=1, concat_a...]
    reshape x7 -> x0, local copies, waits for them, and re-layouts: 121 us -> none  [the longest x2 46.8 us: shards(): arrived.reshape(expert_count, 2, capacity, expert_count, features // expe...]
    all_to_all x3 -> x0, starting transfers between devices: 42.2 us -> none  [the longest x1 18.4 us: shards(): lax.all_to_all(outgoing.reshape(expert_count, 2, capacity, features), 'ex...]
    reduce_sum x1, other arithmetic: 12.4 us -> 45.4 us  [expert_hidden(): jnp.sum(jnp.where((slots[:, :, None] == ids) & hit, weight[:, :, None], 0...]
    ppermute x0 -> x2, waiting for transfers between devices: none -> 26.3 us  [the longest x1 15.7 us: shards(): other = lax.ppermute(own, 'core', [(0, 1), (1, 0)])]
  transfers between devices with their start and end apart: 4 -> 8, of which waited for: 4 -> 8; matrix products, arithmetic and copies ran while one was open for 14% -> 2% of each run, Pallas kernels for 0% -> 0%
where the time goes in v1:
time: 520 us
  waiting for transfers between devices  380 us (73%)
  matrix products  49.5 us (10%)
  other arithmetic  48.9 us (9%)
  blocking collectives  23 us (4%)
  between operations  13.5 us (3%)
    reduce_scatter x3, waiting for transfers between devices, shards(): total = lax.psum_scatter(total, axis, scatter_dimension=0, tiled=True)  173 us
    all_gather x2, waiting for transfers between devices, shards(): own = lax.all_gather(own, axis, axis=0, tiled=True)  156 us
    reduce_sum x1, other arithmetic, expert_hidden(): jnp.sum(jnp.where((slots[:, :, None] == ids) & hit, weight[:, :, None], 0...  45.4 us
    dot_general x2, matrix products, down_project(): lax.dot_general(h, w_down, (((1,), (1,)), ((), ())), preferred_element_ty...  36.8 us
    reduce_scatter x1, waiting for transfers between devices, shards(): lax.psum_scatter(total.astype(jnp.float32), 'z_hi', scatter_dimension=1,...  25.7 us
    all_gather x1, blocking collectives, shards(): own = lax.all_gather(own, axis, axis=0, tiled=True)  18.9 us
    ppermute x1, waiting for transfers between devices, shards(): other = lax.ppermute(own, 'core', [(0, 1), (1, 0)])  15.7 us
    ppermute x1, waiting for transfers between devices, shards(): returned = lax.ppermute(away, 'core', [(0, 1), (1, 0)])  10.5 us
  transfers between devices with their start and end apart: 8, of which 8 were waited for; matrix products, arithmetic and copies ran while one was open for 2% of the time, Pallas kernels for 0%

profile of v1, /device:TPU:1, one launch (start us, length us, event | category | flops | bytes accessed | tf_op | source)
XLA Modules:
  0.0 520.1 jit_solution(11850227993452138166)
XLA Ops:
  6.5 0.7 convert_element_type.36
  7.3 0.1 copy.19
  7.4 0.8 copy.20
  8.1 1.1 concatenate.3
  9.2 18.9 %all_gather.9 = bf16[96,3712]{1,0:T(8,128)(2,1)} all-gather(bf16[24,3712]{1,0:T(8,128)(2,1)S(1)} %constant_dynamic-slice_fusion), channel_id=1, replica_groups=mesh['y'=4,'x'=4,'z_lo'=4,'z_hi'=2,'core'=2] {'z_lo'}, dimensions={0}, use_global_device_ids=true | all-gather | bytes 890880 | tf_op jit(solution)/shard_map/all_gather | solution.py:37
  28.2 0.0 all-gather.5.cloned.1.call-start
  28.2 42.4 %all-gather.3.cloned.1.call-done = bf16[384,3712]{1,0:T(8,128)(2,1)} async-done(((bf16[96,3712]{1,0:T(8,128)(2,1)}), bf16[384,3712]{1,0:T(8,128)(2,1)}) %all-gather.3.cloned.1.call-update) | async-done | bytes 2850832 | tf_op jit(solution)/shard_map/all_gather | solution.py:37
  70.7 0.0 reduce-scatter.5.cloned.1.call-start
  70.8 113.1 %all-gather.5.cloned.1.call-done = bf16[1536,3712]{1,0:T(8,128)(2,1)} async-done(((bf16[384,3712]{1,0:T(8,128)(2,1)}), bf16[1536,3712]{1,0:T(8,128)(2,1)}) %all-gather.5.cloned.1.call-update) | async-done | bytes 11403280 | tf_op jit(solution)/shard_map/all_gather | solution.py:37
  183.8 0.7 collective-permute-start
  184.5 0.1 copy.21
  184.6 0.1 eq.44
  184.8 1.4 slice_convert_fusion.3
  186.2 15.7 %collective-permute-done = bf16[1536,3712]{1,0:T(8,128)(2,1)} collective-permute-done((bf16[1536,3712]{1,0:T(8,128)(2,1)}, bf16[1536,3712]{1,0:T(8,128)(2,1)}, u32[]{:S(2)}, u32[]{:S(2)}) %collective-permute-start) | collective-permute-done | bytes 11403296 | tf_op jit(solution)/shard_map/ppermute | solution.py:38
  202.0 1.3 slice_convert_fusion.1
  203.3 45.4 %select_reduce_fusion.1 = (f32[1536]{0:T(1024)S(1)}, f32[1536]{0:T(1024)S(1)}) fusion(f32[1536,8]{1,0:T(8,128)S(1)} %get-tuple-element.10, f32[1536,8]{1,0:T(8,128)S(1)} %get-tuple-element.9, pred[128]{0:T(512)(128)(4,1)S(1)} %eq.44, f32[1536,8]{1,0:T(8,128)S(1)} %get-tuple-element.8, f32[1536,8]{1,0:T(8,128)S(1)} %get-tuple-element.7), kind=kLoop, calls=%fused_computation.12 | loop fusion | flops 12579840 | bytes 209024 | tf_op jit(solution)/shard_map/reduce_sum | solution.py:15
  248.7 6.3 %fusion = f32[1536,256]{1,0:T(8,128)S(1)} fusion(bf16[1536,3712]{1,0:T(8,128)(2,1)} %collective-permute-done, bf16[1,3,3584,256]{3,2,1,0:T(8,128)(2,1)} %param.7), kind=kOutput, calls=%fused_computation.2 | convolution fusion | flops 2818572288 | bytes 14417920 | tf_op jit(solution)/shard_map/dot_general | solution.py:17
  255.0 17.7 %multiply_convert_fusion = bf16[1536,3584]{1,0:T(8,128)(2,1)} fusion(f32[1536]{0:T(1024)S(1)} %get-tuple-element.6, bf16[1,3,3584,256]{3,2,1,0:T(8,128)(2,1)} %param.7, f32[1536,256]{1,0:T(8,128)S(1)} %fusion, bf16[1536,3712]{1,0:T(8,128)(2,1)} %collective-permute-done), kind=kOutput, calls=%fused_computation.1 | convolution fusion | flops 5650513920 | bytes 27269120 | tf_op jit(solution)/shard_map/dot_general | solution.py:22
  272.7 0.4 collective-permute-start.1
  273.0 6.3 %fusion.6 = f32[1536,256]{1,0:T(8,128)S(1)} fusion(bf16[1536,3712]{1,0:T(8,128)(2,1)} %all-gather.5.cloned.1.call-done, bf16[1,3,3584,256]{3,2,1,0:T(8,128)(2,1)} %param.7), kind=kOutput, calls=%fused_computation.8 | convolution fusion | flops 2818572288 | bytes 14417920 | tf_op jit(solution)/shard_map/dot_general | solution.py:16
  279.4 10.5 %collective-permute-done.1 = bf16[1536,3584]{1,0:T(8,128)(2,1)} collective-permute-done((bf16[1536,3584]{1,0:T(8,128)(2,1)}, bf16[1536,3584]{1,0:T(8,128)(2,1)}, u32[]{:S(2)}, u32[]{:S(2)}) %collective-permute-start.1) | collective-permute-done | bytes 11010080 | tf_op jit(solution)/shard_map/ppermute | solution.py:44
  289.9 19.1 %add_convert_fusion = bf16[1536,3584]{1,0:T(8,128)(2,1)} fusion(bf16[1536,3584]{1,0:T(8,128)(2,1)} %collective-permute-done.1, f32[1536]{0:T(1024)S(1)} %get-tuple-element.5, bf16[1536,3712]{1,0:T(8,128)(2,1)} %all-gather.5.cloned.1.call-done, bf16[1,3,3584,256]{3,2,1,0:T(8,128)(2,1)} %param.7, f32[1536,256]{1,0:T(8,128)S(1)} %fusion.6), kind=kOutput, calls=%fused_computation | convolution fusion | flops 5661523968 | bytes 38279168 | tf_op jit(solution)/shard_map/dot_general | solution.py:22
  309.1 0.0 reduce-scatter.7.cloned.1.call-start
  309.1 105.1 %reduce-scatter.5.cloned.1.call-done = bf16[384,3584]{1,0:T(8,128)(2,1)} async-done(((bf16[1536,3584]{1,0:T(8,128)(2,1)}), bf16[384,3584]{1,0:T(8,128)(2,1)}) %reduce-scatter.5.cloned.1.call-update) | async-done | bytes 2752528 | tf_op jit(solution)/shard_map/reduce_scatter | solution.py:47
  414.3 0.0 reduce-scatter.9.cloned.1.call-start
  414.3 39.8 %reduce-scatter.7.cloned.1.call-done = bf16[96,3584]{1,0:T(8,128)(2,1)} async-done(((bf16[384,3584]{1,0:T(8,128)(2,1)}), bf16[96,3584]{1,0:T(8,128)(2,1)}) %reduce-scatter.7.cloned.1.call-update) | async-done | bytes 688144 | tf_op jit(solution)/shard_map/reduce_scatter | solution.py:47
  454.1 0.0 reduce-scatter.11.cloned.1.call-start
  454.2 27.8 %reduce-scatter.9.cloned.1.call-done = bf16[24,3584]{1,0:T(8,128)(2,1)} async-done(((bf16[96,3584]{1,0:T(8,128)(2,1)}), bf16[24,3584]{1,0:T(8,128)(2,1)}) %reduce-scatter.9.cloned.1.call-update) | async-done | bytes 172048 | tf_op jit(solution)/shard_map/reduce_scatter | solution.py:47
  482.0 25.7 %reduce-scatter.11.cloned.1.call-done = bf16[24,1792]{1,0:T(8,128)(2,1)} async-done(((bf16[24,3584]{1,0:T(8,128)(2,1)}), bf16[24,1792]{1,0:T(8,128)(2,1)}) %reduce-scatter.11.cloned.1.call-update) | async-done | bytes 86032 | tf_op jit(solution)/shard_map/reduce_scatter | solution.py:48
  507.7 0.9 copy.25
  508.6 4.1 all_to_all.19
  512.7 0.6 copy.27
  (14 shorter events, 0.1 us)
Async XLA Ops:
  6.5 178.0 %copy-start.1 = (s32[64]{0:T(128)S(1)}, s32[64]{0:T(128)}, u32[]{:S(2)}) copy-start(s32[64]{0:T(128)} %param.8) | copy-start | bytes 772
  6.5 178.0 %copy-start = (s32[64]{0:T(128)S(1)}, s32[64]{0:T(128)}, u32[]{:S(2)}) copy-start(s32[64]{0:T(128)} %param.9) | copy-start | bytes 772
  6.5 64.1 %all-gather.3.cloned.1.call-start = ((), (), s32[]{:S(2)}) async-start(), calls=%async_computation.5 | async-start | bytes 3563520 | tf_op jit(solution)/shard_map/all_gather | solution.py:37
  28.2 155.6 %all-gather.5.cloned.1.call-start = ((), (), s32[]{:S(2)}) async-start(), calls=%async_computation.6 | async-start | bytes 14254080 | tf_op jit(solution)/shard_map/all_gather | solution.py:37
  70.7 343.6 %reduce-scatter.5.cloned.1.call-start = ((), (), s32[]{:S(2)}) async-start(), calls=%async_computation.7 | async-start | bytes 13762560 | tf_op jit(solution)/shard_map/reduce_scatter | solution.py:47
  183.8 18.1 %collective-permute-start = (bf16[1536,3712]{1,0:T(8,128)(2,1)}, bf16[1536,3712]{1,0:T(8,128)(2,1)}, u32[]{:S(2)}, u32[]{:S(2)}) collective-permute-start(bf16[1536,3712]{1,0:T(8,128)(2,1)} %all-gather.5.cloned.1.call-done), channel_id=1, source_target_pairs={{0,1},{1,0},{2,3},{3,2},{4,5},{5,4},{6,7},{7,6},{8,9},{9,8},{10,11... | collective-permute-start | bytes 34209800 | tf_op jit(solution)/shard_map/ppermute | solution.py:38
  272.7 17.2 %collective-permute-start.1 = (bf16[1536,3584]{1,0:T(8,128)(2,1)}, bf16[1536,3584]{1,0:T(8,128)(2,1)}, u32[]{:S(2)}, u32[]{:S(2)}) collective-permute-start(bf16[1536,3584]{1,0:T(8,128)(2,1)} %multiply_convert_fusion), channel_id=1, source_target_pairs={{0,1},{1,0},{2,3},{3,2},{4,5},{5,4},{6,7},{7,6},{8,9},{9,8},{10,11... | collective-permute-start | bytes 33030152 | tf_op jit(solution)/shard_map/ppermute | solution.py:44
  309.1 145.0 %reduce-scatter.7.cloned.1.call-start = ((), (), s32[]{:S(2)}) async-start(), calls=%async_computation.8 | async-start | bytes 3440640 | tf_op jit(solution)/shard_map/reduce_scatter | solution.py:47
  414.3 67.7 %reduce-scatter.9.cloned.1.call-start = ((), (), s32[]{:S(2)}) async-start(), calls=%async_computation.9 | async-start | bytes 860160 | tf_op jit(solution)/shard_map/reduce_scatter | solution.py:47
  454.1 53.6 %reduce-scatter.11.cloned.1.call-start = ((), (), s32[]{:S(2)}) async-start(), calls=%async_computation.10 | async-start | bytes 258048 | tf_op jit(solution)/shard_map/reduce_scatter | solution.py:48
Sparse Core Ops, SparseCore 0:
  28.3 42.3 all-gather.2
  72.5 111.2 all-gather.4
  309.2 105.0 reduce-scatter.4
  416.7 37.3 reduce-scatter.6
  456.5 25.4 reduce-scatter.8
  484.4 23.2 reduce-scatter.10

commit v2 on v1

v2 whole, which is shorter than its diff:
```python
import jax
import jax.numpy as jnp
import numpy as np
from jax import lax
from jax.sharding import Mesh, PartitionSpec as P

SIDE = 4
OWNER = ("y", "x", "z_lo")
EVERY = ("y", "x", "z_lo", "z_hi", "core")
IDS = np.arange(256).reshape(4, 4, 4, 2, 2)


def axis_rings(along):
    rings = []
    for core in range(2):
        moved = np.moveaxis(IDS[..., core], along[core], -1)
        rings += moved.reshape(-1, SIDE).tolist()
    return rings


SMALL = axis_rings((0, 1))
LARGE = axis_rings((1, 0))


def from_ahead(value, step):
    return lax.ppermute(value, EVERY, [(ring[(i + step) % SIDE], ring[i]) for ring in SMALL for i in range(SIDE)])


def from_behind(value, step):
    return lax.ppermute(value, EVERY, [(ring[i], ring[(i + step) % SIDE]) for ring in SMALL for i in range(SIDE)])


def expert_hidden(packed, features, topk, me, w):
    x = packed[:, :features]
    chosen = packed[:, features:features + topk].astype(jnp.float32)
    weight = packed[:, features + topk:features + 2 * topk].astype(jnp.float32)
    sel = jnp.sum(jnp.where(chosen == me.astype(jnp.float32), weight, 0.0), axis=1)
    g = jnp.dot(x, w[0], preferred_element_type=jnp.float32)
    u = jnp.dot(x, w[1], preferred_element_type=jnp.float32)
    return (jax.nn.silu(g) * u).astype(jnp.bfloat16), sel


def down_project(h, sel, w_down):
    down = lax.dot_general(h, w_down, (((1,), (1,)), ((), ())), preferred_element_type=jnp.float32)
    return down * sel[:, None]


def shards(tokens, expert_weights, partner, replica, routing, gates):
    rows, features = tokens.shape
    topk = routing.shape[1]
    me = lax.axis_index(OWNER)
    core = lax.axis_index("core")
    z_hi = lax.axis_index("z_hi")
    half = rows // 2
    slot_table = jnp.stack([partner, replica], axis=1).reshape(-1)
    named = routing[:, :, None] == jnp.arange(slot_table.shape[0], dtype=jnp.int32)
    chosen = jnp.sum(jnp.where(named, slot_table, 0), axis=2).astype(jnp.bfloat16)
    packed = jnp.concatenate(
        [tokens, chosen, gates, jnp.zeros((rows, 128 - 2 * topk), jnp.bfloat16)], axis=1
    )
    own = lax.dynamic_slice_in_dim(packed, core * half, half, axis=0)
    own = jnp.concatenate(
        [own] + [lax.ppermute(own, "z_lo", [((i + s) % SIDE, i) for i in range(SIDE)]) for s in range(1, SIDE)]
    )
    own = jnp.concatenate([own] + [from_ahead(own, s) for s in range(1, SIDE)])
    own = lax.all_gather(own, EVERY, axis=0, tiled=True, axis_index_groups=LARGE)
    other = lax.ppermute(own, "core", [(0, 1), (1, 0)])
    w = expert_weights[0]
    h_own, sel_own = expert_hidden(own, features, topk, me, w)
    h_other, sel_other = expert_hidden(other, features, topk, me, w)
    away = down_project(h_other, sel_other, w[2]).astype(jnp.bfloat16)
    returned = lax.ppermute(away, "core", [(0, 1), (1, 0)])
    total = (down_project(h_own, sel_own, w[2]) + returned.astype(jnp.float32)).astype(jnp.bfloat16)
    total = lax.psum_scatter(total, EVERY, scatter_dimension=0, tiled=True, axis_index_groups=LARGE)

    parts = total.reshape(SIDE, SIDE * half, features)
    total = parts[0].astype(jnp.float32)
    for s in range(1, SIDE):
        total = total + from_behind(parts[s], s).astype(jnp.float32)
    parts = total.astype(jnp.bfloat16).reshape(SIDE, half, features)
    total = total[:half]
    for s in range(1, SIDE):
        arrived = lax.ppermute(parts[s], "z_lo", [(i, (i + s) % SIDE) for i in range(SIDE)])
        total = total + arrived.astype(jnp.float32)
    wide = features // 2
    sent = lax.dynamic_slice_in_dim(total, (1 - z_hi) * wide, wide, axis=1).astype(jnp.bfloat16)
    arrived = lax.ppermute(sent, "z_hi", [(0, 1), (1, 0)])
    total = lax.dynamic_slice_in_dim(total, z_hi * wide, wide, axis=1) + arrived.astype(jnp.float32)
    return lax.all_to_all(total.astype(jnp.bfloat16), "core", split_axis=1, concat_axis=0, tiled=True)


def solution(mesh):
    grid = Mesh(mesh.devices.reshape(4, 4, 4, 2, 2), EVERY)
    dp = ("z_hi", "core")
    return jax.shard_map(
        shards,
        mesh=grid,
        in_specs=(
            P(OWNER, None),
            P(OWNER, None, None, dp),
            P(),
            P(),
            P(OWNER, None),
            P(OWNER, None),
        ),
        out_specs=P(OWNER, dp),
        check_vma=False,
    )
```

time: 520 us -> 325 us (0.62)
  waiting for transfers between devices: 380 us -> 217 us
  other arithmetic: 48.9 us -> 6.3 us
  starting transfers between devices: 1.25 us -> 23.7 us
  blocking collectives: 23 us -> 6.38 us
    reduce_scatter x4 -> x1, waiting for transfers between devices: 198 us -> 61.2 us  [shards(): lax.psum_scatter(total, EVERY, scatter_dimension=0, tiled=True, axis_inde...]
    all_gather x2 -> x1, waiting for transfers between devices: 156 us -> 67 us  [shards(): lax.all_gather(own, EVERY, axis=0, tiled=True, axis_index_groups=LARGE)]
    ppermute x0 -> x13, waiting for transfers between devices: none -> 62.6 us  [the longest x3 18.1 us: from_ahead(): lax.ppermute(value, EVERY, [(ring[(i + step) % SIDE], ring[i]) for ring i...]
    reduce_sum x1 -> x3, other arithmetic: 45.4 us -> 3.98 us  [the longest x2 3.03 us: expert_hidden(): jnp.sum(jnp.where(chosen == me.astype(jnp.float32), weight, 0.0), axis=1)]
    ppermute x0 -> x13, starting transfers between devices: none -> 22.4 us  [the longest x3 5.63 us: shards(): lax.ppermute(own, 'z_lo', [((i + s) % SIDE, i) for i in range(SIDE)])]
    all_gather x1 -> x0, blocking collectives: 18.9 us -> none  [shards(): own = lax.all_gather(own, axis, axis=0, tiled=True)]
    dot_general x1 -> x0, matrix products: 6.33 us -> none  [expert_hidden(): g = jnp.dot(x, w[0], preferred_element_type=jnp.float32)]
    dot_general x1 -> x2, matrix products: 6.34 us -> 12.7 us  [expert_hidden(): u = jnp.dot(x, w[1], preferred_element_type=jnp.float32)]
  transfers between devices with their start and end apart: 8 -> 17, of which waited for: 8 -> 13; matrix products, arithmetic and copies ran while one was open for 2% -> 2% of each run, Pallas kernels for 0% -> 0%
where the time goes in v2:
time: 325 us; the launch traced here: 324 us
  waiting for transfers between devices  217 us (67%)
  matrix products  49.5 us (15%)
  starting transfers between devices  23.7 us (7%)
  between operations  13.6 us (4%)
  local copies, waits for them, and re-layouts  7.18 us (2%)
  blocking collectives  6.38 us (2%)
  other arithmetic  6.3 us (2%)
    all_gather x1, waiting for transfers between devices, shards(): lax.all_gather(own, EVERY, axis=0, tiled=True, axis_index_groups=LARGE)  67 us
    reduce_scatter x1, waiting for transfers between devices, shards(): lax.psum_scatter(total, EVERY, scatter_dimension=0, tiled=True, axis_inde...  61.2 us
    dot_general x2, matrix products, down_project(): lax.dot_general(h, w_down, (((1,), (1,)), ((), ())), preferred_element_ty...  36.9 us
    ppermute x3, waiting for transfers between devices, from_ahead(): lax.ppermute(value, EVERY, [(ring[(i + step) % SIDE], ring[i]) for ring i...  18.1 us
    ppermute x1, waiting for transfers between devices, shards(): other = lax.ppermute(own, 'core', [(0, 1), (1, 0)])  17.4 us
    ppermute x3, waiting for transfers between devices, from_behind(): lax.ppermute(value, EVERY, [(ring[i], ring[(i + step) % SIDE]) for ring i...  16.9 us
    ppermute x3, waiting for transfers between devices, shards(): lax.ppermute(own, 'z_lo', [((i + s) % SIDE, i) for i in range(SIDE)])  13.9 us
    dot_general x2, matrix products, expert_hidden(): u = jnp.dot(x, w[1], preferred_element_type=jnp.float32)  12.7 us
  transfers between devices with their start and end apart: 17, of which 13 were waited for; matrix products, arithmetic and copies ran while one was open for 2% of the time, Pallas kernels for 0%

profile of v2, /device:TPU:1, one launch (start us, length us, event | category | flops | bytes accessed | tf_op | source)
XLA Modules:
  0.0 324.0 jit_solution(6110925166225685207)
XLA Ops:
  10.0 1.1 concatenate.10
  11.1 5.3 %collective-permute-start = (bf16[24,3712]{1,0:T(8,128)(2,1)S(1)}, bf16[24,3712]{1,0:T(8,128)(2,1)S(1)}, u32[]{:S(2)}, u32[]{:S(2)}) collective-permute-start(bf16[24,3712]{1,0:T(8,128)(2,1)S(1)} %get-tuple-element.8), channel_id=1, source_target_pairs={{4,0},{8,4},{12,8},{0,12},{5,1},{9,5},{13,9},{1,13},{6,2},{10,6},{... | collective-permute-start | bytes 534536 | tf_op jit(solution)/shard_map/ppermute | solution.py:63
  16.7 2.9 collective-permute-done
  19.6 11.0 %collective-permute-done.1 = bf16[24,3712]{1,0:T(8,128)(2,1)S(1)} collective-permute-done((bf16[24,3712]{1,0:T(8,128)(2,1)S(1)}, bf16[24,3712]{1,0:T(8,128)(2,1)S(1)}, u32[]{:S(2)}, u32[]{:S(2)}) %collective-permute-start.1) | collective-permute-done | bytes 178208 | tf_op jit(solution)/shard_map/ppermute | solution.py:63
  30.7 2.6 collective-permute-start.3
  34.4 14.6 %collective-permute-done.3 = bf16[96,3712]{1,0:T(8,128)(2,1)S(1)} collective-permute-done((bf16[96,3712]{1,0:T(8,128)(2,1)S(1)}, bf16[96,3712]{1,0:T(8,128)(2,1)S(1)}, u32[]{:S(2)}, u32[]{:S(2)}) %collective-permute-start.3) | collective-permute-done | bytes 712736 | tf_op jit(solution)/shard_map/ppermute | solution.py:26
  49.2 3.5 %collective-permute-done.5 = bf16[96,3712]{1,0:T(8,128)(2,1)S(1)} collective-permute-done((bf16[96,3712]{1,0:T(8,128)(2,1)S(1)}, bf16[96,3712]{1,0:T(8,128)(2,1)S(1)}, u32[]{:S(2)}, u32[]{:S(2)}) %collective-permute-start.5) | collective-permute-done | bytes 712736 | tf_op jit(solution)/shard_map/ppermute | solution.py:26
  52.8 1.6 copy-done
  54.5 67.0 %all-gather.2.cloned.1.call-done = bf16[1536,3712]{1,0:T(8,128)(2,1)} async-done(((bf16[384,3712]{1,0:T(8,128)(2,1)}), bf16[1536,3712]{1,0:T(8,128)(2,1)}) %all-gather.2.cloned.1.call-update) | async-done | bytes 11403280 | tf_op jit(solution)/shard_map/all_gather | solution.py:66
  122.4 17.4 %collective-permute-done.6 = bf16[1536,3712]{1,0:T(8,128)(2,1)} collective-permute-done((bf16[1536,3712]{1,0:T(8,128)(2,1)}, bf16[1536,3712]{1,0:T(8,128)(2,1)}, u32[]{:S(2)}, u32[]{:S(2)}) %collective-permute-start.6) | collective-permute-done | bytes 11403296 | tf_op jit(solution)/shard_map/ppermute | solution.py:67
  139.8 6.3 %fusion = f32[1536,256]{1,0:T(8,128)S(1)} fusion(bf16[1536,3712]{1,0:T(8,128)(2,1)} %collective-permute-done.6, bf16[1,3,3584,256]{3,2,1,0:T(8,128)(2,1)} %param.7), kind=kOutput, calls=%fused_computation.2 | convolution fusion | flops 2818572288 | bytes 14417920 | tf_op jit(solution)/shard_map/dot_general | solution.py:39
  146.2 1.5 select_reduce_fusion
  147.7 17.6 %multiply_convert_fusion = bf16[1536,3584]{1,0:T(8,128)(2,1)} fusion(f32[1536]{0:T(1024)S(1)} %select_reduce_fusion, bf16[1,3,3584,256]{3,2,1,0:T(8,128)(2,1)} %param.7, f32[1536,256]{1,0:T(8,128)S(1)} %fusion, bf16[1536,3712]{1,0:T(8,128)(2,1)} %collective-permute-done.6), kind=kOutput, calls=%fused_computation.1 | convolution fusion | flops 5650513920 | bytes 27269120 | tf_op jit(solution)/shard_map/dot_general | solution.py:44
  165.7 1.5 select_reduce_fusion.1
  167.2 6.3 %fusion.4 = f32[1536,256]{1,0:T(8,128)S(1)} fusion(bf16[1536,3712]{1,0:T(8,128)(2,1)} %all-gather.2.cloned.1.call-done, bf16[1,3,3584,256]{3,2,1,0:T(8,128)(2,1)} %param.7), kind=kOutput, calls=%fused_computation.6 | convolution fusion | flops 2818572288 | bytes 14417920 | tf_op jit(solution)/shard_map/dot_general | solution.py:39
  173.6 9.0 %collective-permute-done.7 = bf16[1536,3584]{1,0:T(8,128)(2,1)} collective-permute-done((bf16[1536,3584]{1,0:T(8,128)(2,1)}, bf16[1536,3584]{1,0:T(8,128)(2,1)}, u32[]{:S(2)}, u32[]{:S(2)}) %collective-permute-start.7) | collective-permute-done | bytes 11010080 | tf_op jit(solution)/shard_map/ppermute | solution.py:72
  182.6 19.2 %add_convert_fusion = bf16[1536,3584]{1,0:T(8,128)(2,1)} fusion(bf16[1536,3584]{1,0:T(8,128)(2,1)} %collective-permute-done.7, f32[1536]{0:T(1024)S(1)} %select_reduce_fusion.1, bf16[1,3,3584,256]{3,2,1,0:T(8,128)(2,1)} %param.7, f32[1536,256]{1,0:T(8,128)S(1)} %fusion.4, bf16[1536,3712]{1,0:T(8,128)(2,1)} %all-gather.2.cloned.1.call-done), kind=kOutput, calls=%fused_computation | convolution fusion | flops 5661523968 | bytes 38279168 | tf_op jit(solution)/shard_map/dot_general | solution.py:44
  201.8 61.2 %reduce-scatter.2.cloned.1.call-done = bf16[384,3584]{1,0:T(8,128)(2,1)} async-done(((bf16[1536,3584]{1,0:T(8,128)(2,1)}), bf16[384,3584]{1,0:T(8,128)(2,1)}) %reduce-scatter.2.cloned.1.call-update) | async-done | bytes 2752528 | tf_op jit(solution)/shard_map/reduce_scatter | solution.py:74
  263.0 1.6 fusion.46
  264.7 2.2 collective-permute-start.10
  266.9 1.7 collective-permute-start.9
  268.6 13.5 %collective-permute-done.10 = bf16[96,3584]{1,0:T(8,128)(2,1)S(1)} collective-permute-done((bf16[96,3584]{1,0:T(8,128)(2,1)S(1)}, bf16[96,3584]{1,0:T(8,128)(2,1)S(1)}, u32[]{:S(2)}, u32[]{:S(2)}) %collective-permute-start.10) | collective-permute-done | bytes 688160 | tf_op jit(solution)/shard_map/ppermute | solution.py:30
  282.2 3.4 %collective-permute-done.8 = bf16[96,3584]{1,0:T(8,128)(2,1)S(1)} collective-permute-done((bf16[96,3584]{1,0:T(8,128)(2,1)S(1)}, bf16[96,3584]{1,0:T(8,128)(2,1)S(1)}, u32[]{:S(2)}, u32[]{:S(2)}) %collective-permute-start.8) | collective-permute-done | bytes 688160 | tf_op jit(solution)/shard_map/ppermute | solution.py:30
  285.6 1.5 fusion.45
  287.1 1.3 collective-permute-start.11
  288.4 2.3 collective-permute-start.12
  290.7 1.1 collective-permute-start.13
  291.8 1.6 collective-permute-done.11
  293.4 9.3 %collective-permute-done.12 = bf16[24,3584]{1,0:T(8,128)(2,1)S(1)} collective-permute-done((bf16[24,3584]{1,0:T(8,128)(2,1)S(1)}, bf16[24,3584]{1,0:T(8,128)(2,1)S(1)}, u32[]{:S(2)}, u32[]{:S(2)}) %collective-permute-start.12) | collective-permute-done | bytes 172064 | tf_op jit(solution)/shard_map/ppermute | solution.py:83
  302.8 4.5 %collective-permute-start.14 = (bf16[24,1792]{1,0:T(8,128)(2,1)S(1)}, bf16[24,1792]{1,0:T(8,128)(2,1)S(1)}, u32[]{:S(2)}, u32[]{:S(2)}) collective-permute-start(bf16[24,1792]{1,0:T(8,128)(2,1)S(1)} %dynamic-slice_convert_fusion), channel_id=1, source_target_pairs={{0,2},{2,0},{1,3},{3,1},{4,6},{6,4},{5,7},{7,5},{8,10},{10,8},{9,1... | collective-permute-start | bytes 258056 | tf_op jit(solution)/shard_map/ppermute | solution.py:87
  307.2 2.9 collective-permute-done.14
  310.1 6.4 %all_to_all.19 = bf16[24,2,896]{2,0,1:T(8,128)(2,1)S(1)} all-to-all(bf16[24,2,896]{2,0,1:T(8,128)(2,1)S(1)} %bitcast.35), channel_id=1, replica_groups=mesh['y'=4,'x'=4,'z_lo'=4,'z_hi'=2,'core'=2] {'core'}, dimensions={1} | all-to-all | bytes 172032 | tf_op jit(solution)/shard_map/all_to_all | solution.py:89
  (38 shorter events, 7.4 us)
Async XLA Ops:
  6.5 115.0 %all-gather.2.cloned.1.call-start = ((), (), s32[]{:S(2)}) async-start(), calls=%async_computation.2 | async-start | bytes 14254080 | tf_op jit(solution)/shard_map/all_gather | solution.py:66
  11.1 8.5 %collective-permute-start = (bf16[24,3712]{1,0:T(8,128)(2,1)S(1)}, bf16[24,3712]{1,0:T(8,128)(2,1)S(1)}, u32[]{:S(2)}, u32[]{:S(2)}) collective-permute-start(bf16[24,3712]{1,0:T(8,128)(2,1)S(1)} %get-tuple-element.8), channel_id=1, source_target_pairs={{4,0},{8,4},{12,8},{0,12},{5,1},{9,5},{13,9},{1,13},{6,2},{10,6},{... | collective-permute-start | bytes 534536 | tf_op jit(solution)/shard_map/ppermute | solution.py:63
  16.3 14.3 %collective-permute-start.1 = (bf16[24,3712]{1,0:T(8,128)(2,1)S(1)}, bf16[24,3712]{1,0:T(8,128)(2,1)S(1)}, u32[]{:S(2)}, u32[]{:S(2)}) collective-permute-start(bf16[24,3712]{1,0:T(8,128)(2,1)S(1)} %get-tuple-element.8), channel_id=1, source_target_pairs={{8,0},{12,4},{0,8},{4,12},{9,1},{13,5},{1,9},{5,13},{10,2},{14,6},... | collective-permute-start | bytes 534536 | tf_op jit(solution)/shard_map/ppermute | solution.py:63
  16.3 14.3 %collective-permute-start.2 = (bf16[24,3712]{1,0:T(8,128)(2,1)S(1)}, bf16[24,3712]{1,0:T(8,128)(2,1)S(1)}, u32[]{:S(2)}, u32[]{:S(2)}) collective-permute-start(bf16[24,3712]{1,0:T(8,128)(2,1)S(1)} %get-tuple-element.8), channel_id=1, source_target_pairs={{12,0},{0,4},{4,8},{8,12},{13,1},{1,5},{5,9},{9,13},{14,2},{2,6},{... | collective-permute-start | bytes 534536 | tf_op jit(solution)/shard_map/ppermute | solution.py:63
  30.7 18.3 %collective-permute-start.3 = (bf16[96,3712]{1,0:T(8,128)(2,1)S(1)}, bf16[96,3712]{1,0:T(8,128)(2,1)S(1)}, u32[]{:S(2)}, u32[]{:S(2)}) collective-permute-start(bf16[96,3712]{1,0:T(8,128)(2,1)S(1)} %pad_maximum_fusion), channel_id=1, source_target_pairs={{64,0},{128,64},{192,128},{0,192},{66,2},{130,66},{194,130},{2,194... | collective-permute-start | bytes 2138120 | tf_op jit(solution)/shard_map/ppermute | solution.py:26
  33.2 15.9 %collective-permute-start.4 = (bf16[96,3712]{1,0:T(8,128)(2,1)S(1)}, bf16[96,3712]{1,0:T(8,128)(2,1)S(1)}, u32[]{:S(2)}, u32[]{:S(2)}) collective-permute-start(bf16[96,3712]{1,0:T(8,128)(2,1)S(1)} %pad_maximum_fusion), channel_id=1, source_target_pairs={{128,0},{192,64},{0,128},{64,192},{130,2},{194,66},{2,130},{66,194... | collective-permute-start | bytes 2138120 | tf_op jit(solution)/shard_map/ppermute | solution.py:26
  33.7 19.0 %collective-permute-start.5 = (bf16[96,3712]{1,0:T(8,128)(2,1)S(1)}, bf16[96,3712]{1,0:T(8,128)(2,1)S(1)}, u32[]{:S(2)}, u32[]{:S(2)}) collective-permute-start(bf16[96,3712]{1,0:T(8,128)(2,1)S(1)} %pad_maximum_fusion), channel_id=1, source_target_pairs={{192,0},{0,64},{64,128},{128,192},{194,2},{2,66},{66,130},{130,194... | collective-permute-start | bytes 2138120 | tf_op jit(solution)/shard_map/ppermute | solution.py:26
  52.8 1.7 copy-start
  54.5 208.6 %reduce-scatter.2.cloned.1.call-start = ((), (), s32[]{:S(2)}) async-start(), calls=%async_computation.3 | async-start | bytes 13762560 | tf_op jit(solution)/shard_map/reduce_scatter | solution.py:74
  121.6 18.3 %collective-permute-start.6 = (bf16[1536,3712]{1,0:T(8,128)(2,1)}, bf16[1536,3712]{1,0:T(8,128)(2,1)}, u32[]{:S(2)}, u32[]{:S(2)}) collective-permute-start(bf16[1536,3712]{1,0:T(8,128)(2,1)} %all-gather.2.cloned.1.call-done), channel_id=1, source_target_pairs={{0,1},{1,0},{2,3},{3,2},{4,5},{5,4},{6,7},{7,6},{8,9},{9,8},{10,11... | collective-permute-start | bytes 34209800 | tf_op jit(solution)/shard_map/ppermute | solution.py:67
  165.3 17.2 %collective-permute-start.7 = (bf16[1536,3584]{1,0:T(8,128)(2,1)}, bf16[1536,3584]{1,0:T(8,128)(2,1)}, u32[]{:S(2)}, u32[]{:S(2)}) collective-permute-start(bf16[1536,3584]{1,0:T(8,128)(2,1)} %multiply_convert_fusion), channel_id=1, source_target_pairs={{0,1},{1,0},{2,3},{3,2},{4,5},{5,4},{6,7},{7,6},{8,9},{9,8},{10,11... | collective-permute-start | bytes 33030152 | tf_op jit(solution)/shard_map/ppermute | solution.py:72
  264.7 17.5 %collective-permute-start.10 = (bf16[96,3584]{1,0:T(8,128)(2,1)S(1)}, bf16[96,3584]{1,0:T(8,128)(2,1)S(1)}, u32[]{:S(2)}, u32[]{:S(2)}) collective-permute-start(bf16[96,3584]{1,0:T(8,128)(2,1)S(1)} %get-tuple-element.10), channel_id=1, source_target_pairs={{0,192},{64,0},{128,64},{192,128},{2,194},{66,2},{130,66},{194,130... | collective-permute-start | bytes 2064392 | tf_op jit(solution)/shard_map/ppermute | solution.py:30
  266.9 18.7 %collective-permute-start.8 = (bf16[96,3584]{1,0:T(8,128)(2,1)S(1)}, bf16[96,3584]{1,0:T(8,128)(2,1)S(1)}, u32[]{:S(2)}, u32[]{:S(2)}) collective-permute-start(bf16[96,3584]{1,0:T(8,128)(2,1)S(1)} %get-tuple-element.9), channel_id=1, source_target_pairs={{0,64},{64,128},{128,192},{192,0},{2,66},{66,130},{130,194},{194,2... | collective-permute-start | bytes 2064392 | tf_op jit(solution)/shard_map/ppermute | solution.py:30
  266.9 18.7 %collective-permute-start.9 = (bf16[96,3584]{1,0:T(8,128)(2,1)S(1)}, bf16[96,3584]{1,0:T(8,128)(2,1)S(1)}, u32[]{:S(2)}, u32[]{:S(2)}) collective-permute-start(bf16[96,3584]{1,0:T(8,128)(2,1)S(1)} %get-tuple-element.11), channel_id=1, source_target_pairs={{0,128},{64,192},{128,0},{192,64},{2,130},{66,194},{130,2},{194,66... | collective-permute-start | bytes 2064392 | tf_op jit(solution)/shard_map/ppermute | solution.py:30
  287.1 6.3 %collective-permute-start.11 = (bf16[24,3584]{1,0:T(8,128)(2,1)S(1)}, bf16[24,3584]{1,0:T(8,128)(2,1)S(1)}, u32[]{:S(2)}, u32[]{:S(2)}) collective-permute-start(bf16[24,3584]{1,0:T(8,128)(2,1)S(1)} %get-tuple-element.12), channel_id=1, source_target_pairs={{0,4},{4,8},{8,12},{12,0},{1,5},{5,9},{9,13},{13,1},{2,6},{6,10},{... | collective-permute-start | bytes 516104 | tf_op jit(solution)/shard_map/ppermute | solution.py:83
  288.4 14.2 %collective-permute-start.12 = (bf16[24,3584]{1,0:T(8,128)(2,1)S(1)}, bf16[24,3584]{1,0:T(8,128)(2,1)S(1)}, u32[]{:S(2)}, u32[]{:S(2)}) collective-permute-start(bf16[24,3584]{1,0:T(8,128)(2,1)S(1)} %get-tuple-element.14), channel_id=1, source_target_pairs={{0,8},{4,12},{8,0},{12,4},{1,9},{5,13},{9,1},{13,5},{2,10},{6,14},... | collective-permute-start | bytes 516104 | tf_op jit(solution)/shard_map/ppermute | solution.py:83
  290.7 11.9 %collective-permute-start.13 = (bf16[24,3584]{1,0:T(8,128)(2,1)S(1)}, bf16[24,3584]{1,0:T(8,128)(2,1)S(1)}, u32[]{:S(2)}, u32[]{:S(2)}) collective-permute-start(bf16[24,3584]{1,0:T(8,128)(2,1)S(1)} %get-tuple-element.13), channel_id=1, source_target_pairs={{0,12},{4,0},{8,4},{12,8},{1,13},{5,1},{9,5},{13,9},{2,14},{6,2},{... | collective-permute-start | bytes 516104 | tf_op jit(solution)/shard_map/ppermute | solution.py:83
  302.8 7.3 %collective-permute-start.14 = (bf16[24,1792]{1,0:T(8,128)(2,1)S(1)}, bf16[24,1792]{1,0:T(8,128)(2,1)S(1)}, u32[]{:S(2)}, u32[]{:S(2)}) collective-permute-start(bf16[24,1792]{1,0:T(8,128)(2,1)S(1)} %dynamic-slice_convert_fusion), channel_id=1, source_target_pairs={{0,2},{2,0},{1,3},{3,1},{4,6},{6,4},{5,7},{7,5},{8,10},{10,8},{9,1... | collective-permute-start | bytes 258056 | tf_op jit(solution)/shard_map/ppermute | solution.py:87
Sparse Core Ops, SparseCore 0:
  54.6 66.9 all-gather.1
  202.0 61.0 reduce-scatter.1

commit v3 on v2

--- a/solution.py
+++ b/solution.py
@@ -62,18 +62,26 @@
     own = jnp.concatenate(
         [own] + [lax.ppermute(own, "z_lo", [((i + s) % SIDE, i) for i in range(SIDE)]) for s in range(1, SIDE)]
     )
-    own = jnp.concatenate([own] + [from_ahead(own, s) for s in range(1, SIDE)])
-    own = lax.all_gather(own, EVERY, axis=0, tiled=True, axis_index_groups=LARGE)
-    other = lax.ppermute(own, "core", [(0, 1), (1, 0)])
+    near = jnp.concatenate([own, from_ahead(own, 1)])
+    far = jnp.concatenate([from_ahead(own, 2), from_ahead(own, 3)])
     w = expert_weights[0]
-    h_own, sel_own = expert_hidden(own, features, topk, me, w)
-    h_other, sel_other = expert_hidden(other, features, topk, me, w)
-    away = down_project(h_other, sel_other, w[2]).astype(jnp.bfloat16)
-    returned = lax.ppermute(away, "core", [(0, 1), (1, 0)])
-    total = (down_project(h_own, sel_own, w[2]) + returned.astype(jnp.float32)).astype(jnp.bfloat16)
-    total = lax.psum_scatter(total, EVERY, scatter_dimension=0, tiled=True, axis_index_groups=LARGE)
+    first = lax.all_gather(near, EVERY, axis=0, tiled=True, axis_index_groups=LARGE)
+    first, far = lax.optimization_barrier((first, far))
+    second = lax.all_gather(far, EVERY, axis=0, tiled=True, axis_index_groups=LARGE)
+    parts = []
+    for turn in range(2):
+        mine = first if turn == 0 else second
+        other = lax.ppermute(mine, "core", [(0, 1), (1, 0)])
+        h_other, sel_other = expert_hidden(other, features, topk, me, w)
+        away = down_project(h_other, sel_other, w[2]).astype(jnp.bfloat16)
+        returned = lax.ppermute(away, "core", [(0, 1), (1, 0)])
+        h_own, sel_own = expert_hidden(mine, features, topk, me, w)
+        total = (down_project(h_own, sel_own, w[2]) + returned.astype(jnp.float32)).astype(jnp.bfloat16)
+        if turn == 0:
+            total, second = lax.optimization_barrier((total, second))
+        total = lax.psum_scatter(total, EVERY, scatter_dimension=0, tiled=True, axis_index_groups=LARGE)
+        parts += [total[:SIDE * half], total[SIDE * half:]]
 
-    parts = total.reshape(SIDE, SIDE * half, features)
     total = parts[0].astype(jnp.float32)
     for s in range(1, SIDE):
         total = total + from_behind(parts[s], s).astype(jnp.float32)

time: 325 us -> 290 us (0.89)
  waiting for transfers between devices: 217 us -> 153 us
  matrix products: 49.5 us -> 71.5 us
  starting transfers between devices: 23.7 us -> 27 us
  other arithmetic: 6.3 us -> 9.6 us
    all_gather x1 -> x2, waiting for transfers between devices: 67 us -> 24.6 us  [the longest x1 24.6 us: shards(): lax.all_gather(near, EVERY, axis=0, tiled=True, axis_index_groups=LARGE)]
    reduce_scatter x1 -> x2, waiting for transfers between devices: 61.2 us -> 36.9 us  [shards(): lax.psum_scatter(total, EVERY, scatter_dimension=0, tiled=True, axis_inde...]
    dot_general x2 -> x4, matrix products: 36.9 us -> 51.5 us  [down_project(): lax.dot_general(h, w_down, (((1,), (1,)), ((), ())), preferred_element_ty...]
    dot_general x0 -> x2, matrix products: none -> 9.62 us  [expert_hidden(): g = jnp.dot(x, w[0], preferred_element_type=jnp.float32)]
    ppermute x3, waiting for transfers between devices: 18.1 us -> 23.9 us  [from_ahead(): lax.ppermute(value, EVERY, [(ring[(i + step) % SIDE], ring[i]) for ring i...]
    ppermute x1 -> x2, waiting for transfers between devices: 9.02 us -> 6.18 us  [shards(): returned = lax.ppermute(away, 'core', [(0, 1), (1, 0)])]
    ppermute x1 -> x2, waiting for transfers between devices: 17.4 us -> 18.5 us  [shards(): other = lax.ppermute(mine, 'core', [(0, 1), (1, 0)])]
  transfers between devices with their start and end apart: 17 -> 21, of which waited for: 13 -> 16; matrix products, arithmetic and copies ran while one was open for 2% -> 28% of each run, Pallas kernels for 0% -> 0%
where the time goes in v3:
time: 290 us; the launch traced here: 288 us
  waiting for transfers between devices  153 us (53%)
  matrix products  71.5 us (25%)
  starting transfers between devices  27 us (9%)
  between operations  13.3 us (5%)
  other arithmetic  9.6 us (3%)
  local copies, waits for them, and re-layouts  7.37 us (3%)
  blocking collectives  6.34 us (2%)
    dot_general x4, matrix products, down_project(): lax.dot_general(h, w_down, (((1,), (1,)), ((), ())), preferred_element_ty...  51.5 us
    reduce_scatter x2, waiting for transfers between devices, shards(): lax.psum_scatter(total, EVERY, scatter_dimension=0, tiled=True, axis_inde...  36.9 us
    all_gather x1, waiting for transfers between devices, shards(): lax.all_gather(near, EVERY, axis=0, tiled=True, axis_index_groups=LARGE)  24.6 us
    ppermute x3, waiting for transfers between devices, from_ahead(): lax.ppermute(value, EVERY, [(ring[(i + step) % SIDE], ring[i]) for ring i...  23.9 us
    ppermute x2, waiting for transfers between devices, shards(): other = lax.ppermute(mine, 'core', [(0, 1), (1, 0)])  18.5 us
    ppermute x3, waiting for transfers between devices, from_behind(): lax.ppermute(value, EVERY, [(ring[i], ring[(i + step) % SIDE]) for ring i...  15.4 us
    ppermute x3, waiting for transfers between devices, shards(): lax.ppermute(own, 'z_lo', [((i + s) % SIDE, i) for i in range(SIDE)])  13.9 us
    ppermute x3, waiting for transfers between devices, shards(): lax.ppermute(parts[s], 'z_lo', [(i, (i + s) % SIDE) for i in range(SIDE)])  10.9 us
  transfers between devices with their start and end apart: 21, of which 16 were waited for; matrix products, arithmetic and copies ran while one was open for 28% of the time, Pallas kernels for 0%

profile of v3, /device:TPU:1, one launch (start us, length us, event | category | flops | bytes accessed | tf_op | source)
XLA Modules:
  0.0 288.2 jit_solution(33063025484022289)
XLA Ops:
  11.1 5.3 %collective-permute-start = (bf16[24,3712]{1,0:T(8,128)(2,1)S(1)}, bf16[24,3712]{1,0:T(8,128)(2,1)S(1)}, u32[]{:S(2)}, u32[]{:S(2)}) collective-permute-start(bf16[24,3712]{1,0:T(8,128)(2,1)S(1)} %get-tuple-element.16), channel_id=1, source_target_pairs={{4,0},{8,4},{12,8},{0,12},{5,1},{9,5},{13,9},{1,13},{6,2},{10,6},{... | collective-permute-start | bytes 534536 | tf_op jit(solution)/shard_map/ppermute | solution.py:63
  16.7 2.9 collective-permute-done
  19.6 11.0 %collective-permute-done.1 = bf16[24,3712]{1,0:T(8,128)(2,1)S(1)} collective-permute-done((bf16[24,3712]{1,0:T(8,128)(2,1)S(1)}, bf16[24,3712]{1,0:T(8,128)(2,1)S(1)}, u32[]{:S(2)}, u32[]{:S(2)}) %collective-permute-start.1) | collective-permute-done | bytes 178208 | tf_op jit(solution)/shard_map/ppermute | solution.py:63
  30.7 2.6 collective-permute-start.3
  33.3 8.1 %collective-permute-done.3 = bf16[96,3712]{1,0:T(8,128)(2,1)S(1)} collective-permute-done((bf16[96,3712]{1,0:T(8,128)(2,1)S(1)}, bf16[96,3712]{1,0:T(8,128)(2,1)S(1)}, u32[]{:S(2)}, u32[]{:S(2)}) %collective-permute-start.3) | collective-permute-done | bytes 712736 | tf_op jit(solution)/shard_map/ppermute | solution.py:26
  42.6 2.6 collective-permute-start.4
  46.4 8.2 %collective-permute-done.4 = bf16[96,3712]{1,0:T(8,128)(2,1)S(1)} collective-permute-done((bf16[96,3712]{1,0:T(8,128)(2,1)S(1)}, bf16[96,3712]{1,0:T(8,128)(2,1)S(1)}, u32[]{:S(2)}, u32[]{:S(2)}) %collective-permute-start.4) | collective-permute-done | bytes 712736 | tf_op jit(solution)/shard_map/ppermute | solution.py:26
  54.6 7.6 %collective-permute-done.5 = bf16[96,3712]{1,0:T(8,128)(2,1)S(1)} collective-permute-done((bf16[96,3712]{1,0:T(8,128)(2,1)S(1)}, bf16[96,3712]{1,0:T(8,128)(2,1)S(1)}, u32[]{:S(2)}, u32[]{:S(2)}) %collective-permute-start.5) | collective-permute-done | bytes 712736 | tf_op jit(solution)/shard_map/ppermute | solution.py:26
  63.4 24.6 %all-gather.3.cloned.1.call-done = bf16[768,3712]{1,0:T(8,128)(2,1)} async-done(((bf16[192,3712]{1,0:T(8,128)(2,1)}), bf16[768,3712]{1,0:T(8,128)(2,1)}) %all-gather.3.cloned.1.call-update) | async-done | bytes 5701648 | tf_op jit(solution)/shard_map/all_gather | solution.py:68
  88.4 9.2 %collective-permute-done.6 = bf16[768,3712]{1,0:T(8,128)(2,1)} collective-permute-done((bf16[768,3712]{1,0:T(8,128)(2,1)}, bf16[768,3712]{1,0:T(8,128)(2,1)}, u32[]{:S(2)}, u32[]{:S(2)}) %collective-permute-start.6) | collective-permute-done | bytes 5701664 | tf_op jit(solution)/shard_map/ppermute | solution.py:74
  99.0 4.7 %fusion.4 = f32[768,256]{1,0:T(8,128)S(1)} fusion(bf16[768,3712]{1,0:T(8,128)(2,1)} %collective-permute-done.6, bf16[1,3,3584,256]{3,2,1,0:T(8,128)(2,1)} %param.7), kind=kOutput, calls=%fused_computation.8 | convolution fusion | flops 1409286144 | bytes 8126464 | tf_op jit(solution)/shard_map/dot_general | solution.py:39
  103.7 12.6 %multiply_convert_fusion.1 = bf16[768,3584]{1,0:T(8,128)(2,1)} fusion(f32[768]{0:T(1024)S(1)} %select_reduce_fusion.2, bf16[1,3,3584,256]{3,2,1,0:T(8,128)(2,1)} %param.7, f32[768,256]{1,0:T(8,128)S(1)} %fusion.4, bf16[768,3712]{1,0:T(8,128)(2,1)} %collective-permute-done.6), kind=kOutput, calls=%fused_computation.3 | convolution fusion | flops 2825256960 | bytes 15469568 | tf_op jit(solution)/shard_map/dot_general | solution.py:44
  118.0 4.8 %fusion.14 = f32[768,256]{1,0:T(8,128)S(1)} fusion(bf16[768,3712]{1,0:T(8,128)(2,1)} %all-gather.3.cloned.1.call-done, bf16[1,3,3584,256]{3,2,1,0:T(8,128)(2,1)} %param.7), kind=kOutput, calls=%fused_computation.18 | convolution fusion | flops 1409286144 | bytes 8126464 | tf_op jit(solution)/shard_map/dot_general | solution.py:38
  122.8 2.9 collective-permute-done.7
  125.7 13.5 %add_convert_fusion.1 = bf16[768,3584]{1,0:T(8,128)(2,1)} fusion(bf16[768,3584]{1,0:T(8,128)(2,1)} %collective-permute-done.7, f32[768]{0:T(1024)S(1)} %select_reduce_fusion.3, bf16[1,3,3584,256]{3,2,1,0:T(8,128)(2,1)} %param.7, bf16[768,3712]{1,0:T(8,128)(2,1)} %all-gather.3.cloned.1.call-done, f32[768,256]{1,0:T(8,128)S(1)} %fusion.14), kind=kOutput, calls=%fused_computation.2 | convolution fusion | flops 2830761984 | bytes 20974592 | tf_op jit(solution)/shard_map/dot_general | solution.py:44
  139.6 9.2 %collective-permute-done.9 = bf16[768,3712]{1,0:T(8,128)(2,1)} collective-permute-done((bf16[768,3712]{1,0:T(8,128)(2,1)}, bf16[768,3712]{1,0:T(8,128)(2,1)}, u32[]{:S(2)}, u32[]{:S(2)}) %collective-permute-start.9) | collective-permute-done | bytes 5701664 | tf_op jit(solution)/shard_map/ppermute | solution.py:74
  150.1 5.7 %fusion = f32[768,256]{1,0:T(8,128)S(1)} fusion(bf16[768,3712]{1,0:T(8,128)(2,1)} %collective-permute-done.9, bf16[1,3,3584,256]{3,2,1,0:T(8,128)(2,1)} %param.7), kind=kOutput, calls=%fused_computation.4 | convolution fusion | flops 1409286144 | bytes 8126464 | tf_op jit(solution)/shard_map/dot_general | solution.py:39
  155.8 11.9 %multiply_convert_fusion = bf16[768,3584]{1,0:T(8,128)(2,1)} fusion(f32[768]{0:T(1024)S(1)} %select_reduce_fusion, bf16[1,3,3584,256]{3,2,1,0:T(8,128)(2,1)} %param.7, f32[768,256]{1,0:T(8,128)S(1)} %fusion, bf16[768,3712]{1,0:T(8,128)(2,1)} %collective-permute-done.9), kind=kOutput, calls=%fused_computation.1 | convolution fusion | flops 2825256960 | bytes 15469568 | tf_op jit(solution)/shard_map/dot_general | solution.py:44
  169.0 4.8 %fusion.10 = f32[768,256]{1,0:T(8,128)S(1)} fusion(bf16[768,3712]{1,0:T(8,128)(2,1)} %all-gather.5.cloned.1.call-done, bf16[1,3,3584,256]{3,2,1,0:T(8,128)(2,1)} %param.7), kind=kOutput, calls=%fused_computation.14 | convolution fusion | flops 1409286144 | bytes 8126464 | tf_op jit(solution)/shard_map/dot_general | solution.py:38
  173.8 3.3 %collective-permute-done.10 = bf16[768,3584]{1,0:T(8,128)(2,1)} collective-permute-done((bf16[768,3584]{1,0:T(8,128)(2,1)}, bf16[768,3584]{1,0:T(8,128)(2,1)}, u32[]{:S(2)}, u32[]{:S(2)}) %collective-permute-start.10) | collective-permute-done | bytes 5505056 | tf_op jit(solution)/shard_map/ppermute | solution.py:77
  177.1 13.5 %add_convert_fusion = bf16[768,3584]{1,0:T(8,128)(2,1)} fusion(bf16[768,3584]{1,0:T(8,128)(2,1)} %collective-permute-done.10, f32[768]{0:T(1024)S(1)} %select_reduce_fusion.1, bf16[1,3,3584,256]{3,2,1,0:T(8,128)(2,1)} %param.7, bf16[768,3712]{1,0:T(8,128)(2,1)} %all-gather.5.cloned.1.call-done, f32[768,256]{1,0:T(8,128)S(1)} %fusion.10), kind=kOutput, calls=%fused_computation | convolution fusion | flops 2830761984 | bytes 20974592 | tf_op jit(solution)/shard_map/dot_general | solution.py:44
  193.0 36.8 %reduce-scatter.5.cloned.1.call-done = bf16[192,3584]{1,0:T(8,128)(2,1)} async-done(((bf16[768,3584]{1,0:T(8,128)(2,1)}), bf16[192,3584]{1,0:T(8,128)(2,1)}) %reduce-scatter.5.cloned.1.call-update) | async-done | bytes 1376272 | tf_op jit(solution)/shard_map/reduce_scatter | solution.py:82
  231.2 2.5 collective-permute-start.11
  234.6 8.3 %collective-permute-done.11 = bf16[96,3584]{1,0:T(8,128)(2,1)S(1)} collective-permute-done((bf16[96,3584]{1,0:T(8,128)(2,1)S(1)}, bf16[96,3584]{1,0:T(8,128)(2,1)S(1)}, u32[]{:S(2)}, u32[]{:S(2)}) %collective-permute-start.11) | collective-permute-done | bytes 688160 | tf_op jit(solution)/shard_map/ppermute | solution.py:30
  242.9 7.1 %collective-permute-done.12 = bf16[96,3584]{1,0:T(8,128)(2,1)S(1)} collective-permute-done((bf16[96,3584]{1,0:T(8,128)(2,1)S(1)}, bf16[96,3584]{1,0:T(8,128)(2,1)S(1)}, u32[]{:S(2)}, u32[]{:S(2)}) %collective-permute-start.12) | collective-permute-done | bytes 688160 | tf_op jit(solution)/shard_map/ppermute | solution.py:30
  250.1 1.5 fusion.110
  253.0 2.3 collective-permute-start.14
  256.3 1.5 collective-permute-done.13
  257.9 9.3 %collective-permute-done.14 = bf16[24,3584]{1,0:T(8,128)(2,1)S(1)} collective-permute-done((bf16[24,3584]{1,0:T(8,128)(2,1)S(1)}, bf16[24,3584]{1,0:T(8,128)(2,1)S(1)}, u32[]{:S(2)}, u32[]{:S(2)}) %collective-permute-start.14) | collective-permute-done | bytes 172064 | tf_op jit(solution)/shard_map/ppermute | solution.py:91
  267.3 4.5 %collective-permute-start.16 = (bf16[24,1792]{1,0:T(8,128)(2,1)S(1)}, bf16[24,1792]{1,0:T(8,128)(2,1)S(1)}, u32[]{:S(2)}, u32[]{:S(2)}) collective-permute-start(bf16[24,1792]{1,0:T(8,128)(2,1)S(1)} %dynamic-slice_convert_fusion), channel_id=1, source_target_pairs={{0,2},{2,0},{1,3},{3,1},{4,6},{6,4},{5,7},{7,5},{8,10},{10,8},{9,1... | collective-permute-start | bytes 258056 | tf_op jit(solution)/shard_map/ppermute | solution.py:95
  271.8 2.9 collective-permute-done.16
  274.7 6.3 %all_to_all.19 = bf16[24,2,896]{2,0,1:T(8,128)(2,1)S(1)} all-to-all(bf16[24,2,896]{2,0,1:T(8,128)(2,1)S(1)} %bitcast.61), channel_id=1, replica_groups=mesh['y'=4,'x'=4,'z_lo'=4,'z_hi'=2,'core'=2] {'core'}, dimensions={1} | all-to-all | bytes 172032 | tf_op jit(solution)/shard_map/all_to_all | solution.py:97
  (54 shorter events, 23.0 us)
Async XLA Ops:
  6.5 81.5 %all-gather.3.cloned.1.call-start = ((), (), s32[]{:S(2)}) async-start(), calls=%async_computation.3 | async-start | bytes 7127040 | tf_op jit(solution)/shard_map/all_gather | solution.py:68
  11.1 8.5 %collective-permute-start = (bf16[24,3712]{1,0:T(8,128)(2,1)S(1)}, bf16[24,3712]{1,0:T(8,128)(2,1)S(1)}, u32[]{:S(2)}, u32[]{:S(2)}) collective-permute-start(bf16[24,3712]{1,0:T(8,128)(2,1)S(1)} %get-tuple-element.16), channel_id=1, source_target_pairs={{4,0},{8,4},{12,8},{0,12},{5,1},{9,5},{13,9},{1,13},{6,2},{10,6},{... | collective-permute-start | bytes 534536 | tf_op jit(solution)/shard_map/ppermute | solution.py:63
  16.3 14.3 %collective-permute-start.1 = (bf16[24,3712]{1,0:T(8,128)(2,1)S(1)}, bf16[24,3712]{1,0:T(8,128)(2,1)S(1)}, u32[]{:S(2)}, u32[]{:S(2)}) collective-permute-start(bf16[24,3712]{1,0:T(8,128)(2,1)S(1)} %get-tuple-element.16), channel_id=1, source_target_pairs={{8,0},{12,4},{0,8},{4,12},{9,1},{13,5},{1,9},{5,13},{10,2},{14,6},... | collective-permute-start | bytes 534536 | tf_op jit(solution)/shard_map/ppermute | solution.py:63
  16.3 14.3 %collective-permute-start.2 = (bf16[24,3712]{1,0:T(8,128)(2,1)S(1)}, bf16[24,3712]{1,0:T(8,128)(2,1)S(1)}, u32[]{:S(2)}, u32[]{:S(2)}) collective-permute-start(bf16[24,3712]{1,0:T(8,128)(2,1)S(1)} %get-tuple-element.16), channel_id=1, source_target_pairs={{12,0},{0,4},{4,8},{8,12},{13,1},{1,5},{5,9},{9,13},{14,2},{2,6},{... | collective-permute-start | bytes 534536 | tf_op jit(solution)/shard_map/ppermute | solution.py:63
  30.7 10.7 %collective-permute-start.3 = (bf16[96,3712]{1,0:T(8,128)(2,1)S(1)}, bf16[96,3712]{1,0:T(8,128)(2,1)S(1)}, u32[]{:S(2)}, u32[]{:S(2)}) collective-permute-start(bf16[96,3712]{1,0:T(8,128)(2,1)S(1)} %pad_maximum_fusion.1), channel_id=1, source_target_pairs={{64,0},{128,64},{192,128},{0,192},{66,2},{130,66},{194,130},{2,194... | collective-permute-start | bytes 2138120 | tf_op jit(solution)/shard_map/ppermute | solution.py:26
  41.4 1.1 copy-start
  42.6 96.6 %all-gather.5.cloned.1.call-start = ((), (), s32[]{:S(2)}) async-start(), calls=%async_computation.4 | async-start | bytes 7127040 | tf_op jit(solution)/shard_map/all_gather | solution.py:70
  42.6 12.0 %collective-permute-start.4 = (bf16[96,3712]{1,0:T(8,128)(2,1)S(1)}, bf16[96,3712]{1,0:T(8,128)(2,1)S(1)}, u32[]{:S(2)}, u32[]{:S(2)}) collective-permute-start(bf16[96,3712]{1,0:T(8,128)(2,1)S(1)} %pad_maximum_fusion.1), channel_id=1, source_target_pairs={{128,0},{192,64},{0,128},{64,192},{130,2},{194,66},{2,130},{66,194... | collective-permute-start | bytes 2138120 | tf_op jit(solution)/shard_map/ppermute | solution.py:26
  45.2 17.0 %collective-permute-start.5 = (bf16[96,3712]{1,0:T(8,128)(2,1)S(1)}, bf16[96,3712]{1,0:T(8,128)(2,1)S(1)}, u32[]{:S(2)}, u32[]{:S(2)}) collective-permute-start(bf16[96,3712]{1,0:T(8,128)(2,1)S(1)} %pad_maximum_fusion.1), channel_id=1, source_target_pairs={{192,0},{0,64},{64,128},{128,192},{194,2},{2,66},{66,130},{130,194... | collective-permute-start | bytes 2138120 | tf_op jit(solution)/shard_map/ppermute | solution.py:26
  88.0 9.7 %collective-permute-start.6 = (bf16[768,3712]{1,0:T(8,128)(2,1)}, bf16[768,3712]{1,0:T(8,128)(2,1)}, u32[]{:S(2)}, u32[]{:S(2)}) collective-permute-start(bf16[768,3712]{1,0:T(8,128)(2,1)} %all-gather.3.cloned.1.call-done), channel_id=1, source_target_pairs={{0,1},{1,0},{2,3},{3,2},{4,5},{5,4},{6,7},{7,6},{8,9},{9,8},{10,11... | collective-permute-start | bytes 17104904 | tf_op jit(solution)/shard_map/ppermute | solution.py:74
  88.4 102.2 %reduce-scatter.3.cloned.1.call-start = ((), (), s32[]{:S(2)}) async-start(), calls=%async_computation.5 | async-start | bytes 6881280 | tf_op jit(solution)/shard_map/reduce_scatter | solution.py:82
  116.3 9.4 %collective-permute-start.7 = (bf16[768,3584]{1,0:T(8,128)(2,1)}, bf16[768,3584]{1,0:T(8,128)(2,1)}, u32[]{:S(2)}, u32[]{:S(2)}) collective-permute-start(bf16[768,3584]{1,0:T(8,128)(2,1)} %multiply_convert_fusion.1), channel_id=1, source_target_pairs={{0,1},{1,0},{2,3},{3,2},{4,5},{5,4},{6,7},{7,6},{8,9},{9,8},{10,11... | collective-permute-start | bytes 16515080 | tf_op jit(solution)/shard_map/ppermute | solution.py:77
  139.2 9.7 %collective-permute-start.9 = (bf16[768,3712]{1,0:T(8,128)(2,1)}, bf16[768,3712]{1,0:T(8,128)(2,1)}, u32[]{:S(2)}, u32[]{:S(2)}) collective-permute-start(bf16[768,3712]{1,0:T(8,128)(2,1)} %all-gather.5.cloned.1.call-done), channel_id=1, source_target_pairs={{0,1},{1,0},{2,3},{3,2},{4,5},{5,4},{6,7},{7,6},{8,9},{9,8},{10,11... | collective-permute-start | bytes 17104904 | tf_op jit(solution)/shard_map/ppermute | solution.py:74
  139.6 90.3 %reduce-scatter.5.cloned.1.call-start = ((), (), s32[]{:S(2)}) async-start(), calls=%async_computation.6 | async-start | bytes 6881280 | tf_op jit(solution)/shard_map/reduce_scatter | solution.py:82
  167.7 9.4 %collective-permute-start.10 = (bf16[768,3584]{1,0:T(8,128)(2,1)}, bf16[768,3584]{1,0:T(8,128)(2,1)}, u32[]{:S(2)}, u32[]{:S(2)}) collective-permute-start(bf16[768,3584]{1,0:T(8,128)(2,1)} %multiply_convert_fusion), channel_id=1, source_target_pairs={{0,1},{1,0},{2,3},{3,2},{4,5},{5,4},{6,7},{7,6},{8,9},{9,8},{10,11... | collective-permute-start | bytes 16515080 | tf_op jit(solution)/shard_map/ppermute | solution.py:77
  191.8 42.8 %collective-permute-start.8 = (bf16[96,3584]{1,0:T(8,128)(2,1)S(1)}, bf16[96,3584]{1,0:T(8,128)(2,1)S(1)}, u32[]{:S(2)}, u32[]{:S(2)}) collective-permute-start(bf16[96,3584]{1,0:T(8,128)(2,1)S(1)} %slice.111), channel_id=1, source_target_pairs={{0,64},{64,128},{128,192},{192,0},{2,66},{66,130},{130,194},{194,2... | collective-permute-start | bytes 2064392 | tf_op jit(solution)/shard_map/ppermute | solution.py:30
  231.2 11.7 %collective-permute-start.11 = (bf16[96,3584]{1,0:T(8,128)(2,1)S(1)}, bf16[96,3584]{1,0:T(8,128)(2,1)S(1)}, u32[]{:S(2)}, u32[]{:S(2)}) collective-permute-start(bf16[96,3584]{1,0:T(8,128)(2,1)S(1)} %get-tuple-element.17), channel_id=1, source_target_pairs={{0,128},{64,192},{128,0},{192,64},{2,130},{66,194},{130,2},{194,66... | collective-permute-start | bytes 2064392 | tf_op jit(solution)/shard_map/ppermute | solution.py:30
  233.7 16.3 %collective-permute-start.12 = (bf16[96,3584]{1,0:T(8,128)(2,1)S(1)}, bf16[96,3584]{1,0:T(8,128)(2,1)S(1)}, u32[]{:S(2)}, u32[]{:S(2)}) collective-permute-start(bf16[96,3584]{1,0:T(8,128)(2,1)S(1)} %get-tuple-element.18), channel_id=1, source_target_pairs={{0,192},{64,0},{128,64},{192,128},{2,194},{66,2},{130,66},{194,130... | collective-permute-start | bytes 2064392 | tf_op jit(solution)/shard_map/ppermute | solution.py:30
  251.6 6.3 %collective-permute-start.13 = (bf16[24,3584]{1,0:T(8,128)(2,1)S(1)}, bf16[24,3584]{1,0:T(8,128)(2,1)S(1)}, u32[]{:S(2)}, u32[]{:S(2)}) collective-permute-start(bf16[24,3584]{1,0:T(8,128)(2,1)S(1)} %get-tuple-element.19), channel_id=1, source_target_pairs={{0,4},{4,8},{8,12},{12,0},{1,5},{5,9},{9,13},{13,1},{2,6},{6,10},{... | collective-permute-start | bytes 516104 | tf_op jit(solution)/shard_map/ppermute | solution.py:91
  253.0 14.3 %collective-permute-start.14 = (bf16[24,3584]{1,0:T(8,128)(2,1)S(1)}, bf16[24,3584]{1,0:T(8,128)(2,1)S(1)}, u32[]{:S(2)}, u32[]{:S(2)}) collective-permute-start(bf16[24,3584]{1,0:T(8,128)(2,1)S(1)} %get-tuple-element.21), channel_id=1, source_target_pairs={{0,8},{4,12},{8,0},{12,4},{1,9},{5,13},{9,1},{13,5},{2,10},{6,14},... | collective-permute-start | bytes 516104 | tf_op jit(solution)/shard_map/ppermute | solution.py:91
  255.2 12.0 %collective-permute-start.15 = (bf16[24,3584]{1,0:T(8,128)(2,1)S(1)}, bf16[24,3584]{1,0:T(8,128)(2,1)S(1)}, u32[]{:S(2)}, u32[]{:S(2)}) collective-permute-start(bf16[24,3584]{1,0:T(8,128)(2,1)S(1)} %get-tuple-element.20), channel_id=1, source_target_pairs={{0,12},{4,0},{8,4},{12,8},{1,13},{5,1},{9,5},{13,9},{2,14},{6,2},{... | collective-permute-start | bytes 516104 | tf_op jit(solution)/shard_map/ppermute | solution.py:91
  267.3 7.3 %collective-permute-start.16 = (bf16[24,1792]{1,0:T(8,128)(2,1)S(1)}, bf16[24,1792]{1,0:T(8,128)(2,1)S(1)}, u32[]{:S(2)}, u32[]{:S(2)}) collective-permute-start(bf16[24,1792]{1,0:T(8,128)(2,1)S(1)} %dynamic-slice_convert_fusion), channel_id=1, source_target_pairs={{0,2},{2,0},{1,3},{3,1},{4,6},{6,4},{5,7},{7,5},{8,10},{10,8},{9,1... | collective-permute-start | bytes 258056 | tf_op jit(solution)/shard_map/ppermute | solution.py:95
Sparse Core Ops, SparseCore 0:
  42.7 45.2 all-gather.2
  89.8 41.5 all-gather.4
  139.7 39.0 reduce-scatter.2
  190.7 39.0 reduce-scatter.4

commit v4 on v3

--- a/solution.py
+++ b/solution.py
@@ -85,15 +85,16 @@
     total = parts[0].astype(jnp.float32)
     for s in range(1, SIDE):
         total = total + from_behind(parts[s], s).astype(jnp.float32)
-    parts = total.astype(jnp.bfloat16).reshape(SIDE, half, features)
-    total = total[:half]
-    for s in range(1, SIDE):
-        arrived = lax.ppermute(parts[s], "z_lo", [(i, (i + s) % SIDE) for i in range(SIDE)])
-        total = total + arrived.astype(jnp.float32)
     wide = features // 2
-    sent = lax.dynamic_slice_in_dim(total, (1 - z_hi) * wide, wide, axis=1).astype(jnp.bfloat16)
-    arrived = lax.ppermute(sent, "z_hi", [(0, 1), (1, 0)])
-    total = lax.dynamic_slice_in_dim(total, z_hi * wide, wide, axis=1) + arrived.astype(jnp.float32)
+    here = lax.dynamic_slice_in_dim(total, z_hi * wide, wide, axis=1)
+    there = lax.dynamic_slice_in_dim(total, (1 - z_hi) * wide, wide, axis=1)
+    total = here[:half]
+    for s in range(SIDE):
+        for flip, source in ((0, here), (1, there)):
+            if s or flip:
+                sent = source[s * half:(s + 1) * half].astype(jnp.bfloat16)
+                route = [(2 * i + j, 2 * ((i + s) % SIDE) + (j ^ flip)) for i in range(SIDE) for j in range(2)]
+                total = total + lax.ppermute(sent, ("z_lo", "z_hi"), route).astype(jnp.float32)
     return lax.all_to_all(total.astype(jnp.bfloat16), "core", split_axis=1, concat_axis=0, tiled=True)
 
 

time: 290 us -> 287 us (0.990)
    ppermute x4 -> x7, starting transfers between devices: 9.17 us -> 11.6 us  [shards(): lax.ppermute(sent, ('z_lo', 'z_hi'), route).astype(jnp.float32)]
    ppermute x4 -> x7, waiting for transfers between devices: 13.8 us -> 11.5 us  [shards(): lax.ppermute(sent, ('z_lo', 'z_hi'), route).astype(jnp.float32)]
  transfers between devices with their start and end apart: 21 -> 24, of which waited for: 16 -> 17; matrix products, arithmetic and copies ran while one was open for 28% -> 28% of each run, Pallas kernels for 0% -> 0%
where the time goes in v4:
time: 287 us
  waiting for transfers between devices  151 us (53%)
  matrix products  71.5 us (25%)
  starting transfers between devices  29.4 us (10%)
  between operations  13.3 us (5%)
  other arithmetic  9.69 us (3%)
  local copies, waits for them, and re-layouts  7.45 us (3%)
  blocking collectives  4.4 us (2%)
    dot_general x4, matrix products, down_project(): lax.dot_general(h, w_down, (((1,), (1,)), ((), ())), preferred_element_ty...  51.4 us
    reduce_scatter x2, waiting for transfers between devices, shards(): lax.psum_scatter(total, EVERY, scatter_dimension=0, tiled=True, axis_inde...  36.9 us
    all_gather x1, waiting for transfers between devices, shards(): lax.all_gather(near, EVERY, axis=0, tiled=True, axis_index_groups=LARGE)  24.6 us
    ppermute x3, waiting for transfers between devices, from_ahead(): lax.ppermute(value, EVERY, [(ring[(i + step) % SIDE], ring[i]) for ring i...  23.9 us
    ppermute x2, waiting for transfers between devices, shards(): other = lax.ppermute(mine, 'core', [(0, 1), (1, 0)])  18.5 us
    ppermute x3, waiting for transfers between devices, from_behind(): lax.ppermute(value, EVERY, [(ring[i], ring[(i + step) % SIDE]) for ring i...  15.5 us
    ppermute x3, waiting for transfers between devices, shards(): lax.ppermute(own, 'z_lo', [((i + s) % SIDE, i) for i in range(SIDE)])  13.9 us
    ppermute x7, starting transfers between devices, shards(): lax.ppermute(sent, ('z_lo', 'z_hi'), route).astype(jnp.float32)  11.6 us
  transfers between devices with their start and end apart: 24, of which 17 were waited for; matrix products, arithmetic and copies ran while one was open for 28% of the time, Pallas kernels for 0%

profile of v4, /device:TPU:1, one launch (start us, length us, event | category | flops | bytes accessed | tf_op | source)
XLA Modules:
  0.0 286.7 jit_solution(3301914076530359987)
XLA Ops:
  11.1 5.3 %collective-permute-start = (bf16[24,3712]{1,0:T(8,128)(2,1)S(1)}, bf16[24,3712]{1,0:T(8,128)(2,1)S(1)}, u32[]{:S(2)}, u32[]{:S(2)}) collective-permute-start(bf16[24,3712]{1,0:T(8,128)(2,1)S(1)} %get-tuple-element.14), channel_id=1, source_target_pairs={{4,0},{8,4},{12,8},{0,12},{5,1},{9,5},{13,9},{1,13},{6,2},{10,6},{... | collective-permute-start | bytes 534536 | tf_op jit(solution)/shard_map/ppermute | solution.py:63
  16.7 2.9 %collective-permute-done = bf16[24,3712]{1,0:T(8,128)(2,1)S(1)} collective-permute-done((bf16[24,3712]{1,0:T(8,128)(2,1)S(1)}, bf16[24,3712]{1,0:T(8,128)(2,1)S(1)}, u32[]{:S(2)}, u32[]{:S(2)}) %collective-permute-start) | collective-permute-done | bytes 178208 | tf_op jit(solution)/shard_map/ppermute | solution.py:63
  19.6 11.0 %collective-permute-done.1 = bf16[24,3712]{1,0:T(8,128)(2,1)S(1)} collective-permute-done((bf16[24,3712]{1,0:T(8,128)(2,1)S(1)}, bf16[24,3712]{1,0:T(8,128)(2,1)S(1)}, u32[]{:S(2)}, u32[]{:S(2)}) %collective-permute-start.1) | collective-permute-done | bytes 178208 | tf_op jit(solution)/shard_map/ppermute | solution.py:63
  30.7 2.6 collective-permute-start.3
  33.3 8.1 %collective-permute-done.3 = bf16[96,3712]{1,0:T(8,128)(2,1)S(1)} collective-permute-done((bf16[96,3712]{1,0:T(8,128)(2,1)S(1)}, bf16[96,3712]{1,0:T(8,128)(2,1)S(1)}, u32[]{:S(2)}, u32[]{:S(2)}) %collective-permute-start.3) | collective-permute-done | bytes 712736 | tf_op jit(solution)/shard_map/ppermute | solution.py:26
  42.6 2.6 collective-permute-start.4
  46.4 8.2 %collective-permute-done.4 = bf16[96,3712]{1,0:T(8,128)(2,1)S(1)} collective-permute-done((bf16[96,3712]{1,0:T(8,128)(2,1)S(1)}, bf16[96,3712]{1,0:T(8,128)(2,1)S(1)}, u32[]{:S(2)}, u32[]{:S(2)}) %collective-permute-start.4) | collective-permute-done | bytes 712736 | tf_op jit(solution)/shard_map/ppermute | solution.py:26
  54.6 7.6 %collective-permute-done.5 = bf16[96,3712]{1,0:T(8,128)(2,1)S(1)} collective-permute-done((bf16[96,3712]{1,0:T(8,128)(2,1)S(1)}, bf16[96,3712]{1,0:T(8,128)(2,1)S(1)}, u32[]{:S(2)}, u32[]{:S(2)}) %collective-permute-start.5) | collective-permute-done | bytes 712736 | tf_op jit(solution)/shard_map/ppermute | solution.py:26
  63.4 24.6 %all-gather.3.cloned.1.call-done = bf16[768,3712]{1,0:T(8,128)(2,1)} async-done(((bf16[192,3712]{1,0:T(8,128)(2,1)}), bf16[768,3712]{1,0:T(8,128)(2,1)}) %all-gather.3.cloned.1.call-update) | async-done | bytes 5701648 | tf_op jit(solution)/shard_map/all_gather | solution.py:68
  88.4 9.2 %collective-permute-done.6 = bf16[768,3712]{1,0:T(8,128)(2,1)} collective-permute-done((bf16[768,3712]{1,0:T(8,128)(2,1)}, bf16[768,3712]{1,0:T(8,128)(2,1)}, u32[]{:S(2)}, u32[]{:S(2)}) %collective-permute-start.6) | collective-permute-done | bytes 5701664 | tf_op jit(solution)/shard_map/ppermute | solution.py:74
  98.9 4.7 %fusion.4 = f32[768,256]{1,0:T(8,128)S(1)} fusion(bf16[768,3712]{1,0:T(8,128)(2,1)} %collective-permute-done.6, bf16[1,3,3584,256]{3,2,1,0:T(8,128)(2,1)} %param.7), kind=kOutput, calls=%fused_computation.8 | convolution fusion | flops 1409286144 | bytes 8126464 | tf_op jit(solution)/shard_map/dot_general | solution.py:39
  103.7 12.6 %multiply_convert_fusion.1 = bf16[768,3584]{1,0:T(8,128)(2,1)} fusion(f32[768]{0:T(1024)S(1)} %select_reduce_fusion.2, bf16[1,3,3584,256]{3,2,1,0:T(8,128)(2,1)} %param.7, f32[768,256]{1,0:T(8,128)S(1)} %fusion.4, bf16[768,3712]{1,0:T(8,128)(2,1)} %collective-permute-done.6), kind=kOutput, calls=%fused_computation.3 | convolution fusion | flops 2825256960 | bytes 15469568 | tf_op jit(solution)/shard_map/dot_general | solution.py:44
  117.9 4.8 %fusion.14 = f32[768,256]{1,0:T(8,128)S(1)} fusion(bf16[768,3712]{1,0:T(8,128)(2,1)} %all-gather.3.cloned.1.call-done, bf16[1,3,3584,256]{3,2,1,0:T(8,128)(2,1)} %param.7), kind=kOutput, calls=%fused_computation.18 | convolution fusion | flops 1409286144 | bytes 8126464 | tf_op jit(solution)/shard_map/dot_general | solution.py:38
  122.8 2.9 %collective-permute-done.7 = bf16[768,3584]{1,0:T(8,128)(2,1)} collective-permute-done((bf16[768,3584]{1,0:T(8,128)(2,1)}, bf16[768,3584]{1,0:T(8,128)(2,1)}, u32[]{:S(2)}, u32[]{:S(2)}) %collective-permute-start.7) | collective-permute-done | bytes 5505056 | tf_op jit(solution)/shard_map/ppermute | solution.py:77
  125.7 13.5 %add_convert_fusion.1 = bf16[768,3584]{1,0:T(8,128)(2,1)} fusion(bf16[768,3584]{1,0:T(8,128)(2,1)} %collective-permute-done.7, f32[768]{0:T(1024)S(1)} %select_reduce_fusion.3, bf16[1,3,3584,256]{3,2,1,0:T(8,128)(2,1)} %param.7, bf16[768,3712]{1,0:T(8,128)(2,1)} %all-gather.3.cloned.1.call-done, f32[768,256]{1,0:T(8,128)S(1)} %fusion.14), kind=kOutput, calls=%fused_computation.2 | convolution fusion | flops 2830761984 | bytes 20974592 | tf_op jit(solution)/shard_map/dot_general | solution.py:44
  139.6 9.2 %collective-permute-done.9 = bf16[768,3712]{1,0:T(8,128)(2,1)} collective-permute-done((bf16[768,3712]{1,0:T(8,128)(2,1)}, bf16[768,3712]{1,0:T(8,128)(2,1)}, u32[]{:S(2)}, u32[]{:S(2)}) %collective-permute-start.9) | collective-permute-done | bytes 5701664 | tf_op jit(solution)/shard_map/ppermute | solution.py:74
  150.1 5.7 %fusion = f32[768,256]{1,0:T(8,128)S(1)} fusion(bf16[768,3712]{1,0:T(8,128)(2,1)} %collective-permute-done.9, bf16[1,3,3584,256]{3,2,1,0:T(8,128)(2,1)} %param.7), kind=kOutput, calls=%fused_computation.4 | convolution fusion | flops 1409286144 | bytes 8126464 | tf_op jit(solution)/shard_map/dot_general | solution.py:39
  155.8 11.9 %multiply_convert_fusion = bf16[768,3584]{1,0:T(8,128)(2,1)} fusion(f32[768]{0:T(1024)S(1)} %select_reduce_fusion, bf16[1,3,3584,256]{3,2,1,0:T(8,128)(2,1)} %param.7, f32[768,256]{1,0:T(8,128)S(1)} %fusion, bf16[768,3712]{1,0:T(8,128)(2,1)} %collective-permute-done.9), kind=kOutput, calls=%fused_computation.1 | convolution fusion | flops 2825256960 | bytes 15469568 | tf_op jit(solution)/shard_map/dot_general | solution.py:44
  169.0 4.8 %fusion.10 = f32[768,256]{1,0:T(8,128)S(1)} fusion(bf16[768,3712]{1,0:T(8,128)(2,1)} %all-gather.5.cloned.1.call-done, bf16[1,3,3584,256]{3,2,1,0:T(8,128)(2,1)} %param.7), kind=kOutput, calls=%fused_computation.14 | convolution fusion | flops 1409286144 | bytes 8126464 | tf_op jit(solution)/shard_map/dot_general | solution.py:38
  173.8 3.3 %collective-permute-done.10 = bf16[768,3584]{1,0:T(8,128)(2,1)} collective-permute-done((bf16[768,3584]{1,0:T(8,128)(2,1)}, bf16[768,3584]{1,0:T(8,128)(2,1)}, u32[]{:S(2)}, u32[]{:S(2)}) %collective-permute-start.10) | collective-permute-done | bytes 5505056 | tf_op jit(solution)/shard_map/ppermute | solution.py:77
  177.1 13.5 %add_convert_fusion = bf16[768,3584]{1,0:T(8,128)(2,1)} fusion(bf16[768,3584]{1,0:T(8,128)(2,1)} %collective-permute-done.10, f32[768]{0:T(1024)S(1)} %select_reduce_fusion.1, bf16[1,3,3584,256]{3,2,1,0:T(8,128)(2,1)} %param.7, bf16[768,3712]{1,0:T(8,128)(2,1)} %all-gather.5.cloned.1.call-done, f32[768,256]{1,0:T(8,128)S(1)} %fusion.10), kind=kOutput, calls=%fused_computation | convolution fusion | flops 2830761984 | bytes 20974592 | tf_op jit(solution)/shard_map/dot_general | solution.py:44
  193.0 36.8 %reduce-scatter.5.cloned.1.call-done = bf16[192,3584]{1,0:T(8,128)(2,1)} async-done(((bf16[768,3584]{1,0:T(8,128)(2,1)}), bf16[192,3584]{1,0:T(8,128)(2,1)}) %reduce-scatter.5.cloned.1.call-update) | async-done | bytes 1376272 | tf_op jit(solution)/shard_map/reduce_scatter | solution.py:82
  231.2 2.5 collective-permute-start.11
  234.6 8.3 %collective-permute-done.11 = bf16[96,3584]{1,0:T(8,128)(2,1)S(1)} collective-permute-done((bf16[96,3584]{1,0:T(8,128)(2,1)S(1)}, bf16[96,3584]{1,0:T(8,128)(2,1)S(1)}, u32[]{:S(2)}, u32[]{:S(2)}) %collective-permute-start.11) | collective-permute-done | bytes 688160 | tf_op jit(solution)/shard_map/ppermute | solution.py:30
  242.9 7.2 %collective-permute-done.12 = bf16[96,3584]{1,0:T(8,128)(2,1)} collective-permute-done((bf16[96,3584]{1,0:T(8,128)(2,1)S(1)}, bf16[96,3584]{1,0:T(8,128)(2,1)}, u32[]{:S(2)}, u32[]{:S(2)}) %collective-permute-start.12) | collective-permute-done | bytes 688160 | tf_op jit(solution)/shard_map/ppermute | solution.py:30
  251.9 5.5 %collective-permute-start.13 = (bf16[24,1792]{1,0:T(8,128)(2,1)S(1)}, bf16[24,1792]{1,0:T(8,128)(2,1)S(1)}, u32[]{:S(2)}, u32[]{:S(2)}) collective-permute-start(bf16[24,1792]{1,0:T(8,128)(2,1)S(1)} %get-tuple-element.19), channel_id=1, source_target_pairs={{0,2},{2,0},{4,6},{6,4},{8,10},{10,8},{12,14},{14,12},{1,3},{3,1},... | collective-permute-start | bytes 258056 | tf_op jit(solution)/shard_map/ppermute | solution.py:97
  257.5 2.9 %collective-permute-start.17 = (bf16[24,1792]{1,0:T(8,128)(2,1)S(1)}, bf16[24,1792]{1,0:T(8,128)(2,1)S(1)}, u32[]{:S(2)}, u32[]{:S(2)}) collective-permute-start(bf16[24,1792]{1,0:T(8,128)(2,1)S(1)} %get-tuple-element.21), channel_id=1, source_target_pairs={{0,10},{2,8},{4,14},{6,12},{8,2},{10,0},{12,6},{14,4},{1,11},{3,9}... | collective-permute-start | bytes 258056 | tf_op jit(solution)/shard_map/ppermute | solution.py:97
  261.2 2.2 collective-permute-start.14
  263.5 3.7 %collective-permute-done.15 = bf16[24,1792]{1,0:T(8,128)(2,1)S(1)} collective-permute-done((bf16[24,1792]{1,0:T(8,128)(2,1)S(1)}, bf16[24,1792]{1,0:T(8,128)(2,1)S(1)}, u32[]{:S(2)}, u32[]{:S(2)}) %collective-permute-start.15) | collective-permute-done | bytes 86048 | tf_op jit(solution)/shard_map/ppermute | solution.py:97
  267.2 3.5 %collective-permute-done.17 = bf16[24,1792]{1,0:T(8,128)(2,1)S(1)} collective-permute-done((bf16[24,1792]{1,0:T(8,128)(2,1)S(1)}, bf16[24,1792]{1,0:T(8,128)(2,1)S(1)}, u32[]{:S(2)}, u32[]{:S(2)}) %collective-permute-start.17) | collective-permute-done | bytes 86048 | tf_op jit(solution)/shard_map/ppermute | solution.py:97
  272.6 2.4 collective-permute-done.18
  275.1 4.4 %all_to_all.19 = bf16[24,2,896]{2,0,1:T(8,128)(2,1)S(1)} all-to-all(bf16[24,2,896]{2,0,1:T(8,128)(2,1)S(1)} %bitcast.61), channel_id=1, replica_groups=mesh['y'=4,'x'=4,'z_lo'=4,'z_hi'=2,'core'=2] {'core'}, dimensions={1} | all-to-all | bytes 172032 | tf_op jit(solution)/shard_map/all_to_all | solution.py:98
  (60 shorter events, 25.0 us)
Async XLA Ops:
  6.5 81.5 %all-gather.3.cloned.1.call-start = ((), (), s32[]{:S(2)}) async-start(), calls=%async_computation.3 | async-start | bytes 7127040 | tf_op jit(solution)/shard_map/all_gather | solution.py:68
  11.1 8.5 %collective-permute-start = (bf16[24,3712]{1,0:T(8,128)(2,1)S(1)}, bf16[24,3712]{1,0:T(8,128)(2,1)S(1)}, u32[]{:S(2)}, u32[]{:S(2)}) collective-permute-start(bf16[24,3712]{1,0:T(8,128)(2,1)S(1)} %get-tuple-element.14), channel_id=1, source_target_pairs={{4,0},{8,4},{12,8},{0,12},{5,1},{9,5},{13,9},{1,13},{6,2},{10,6},{... | collective-permute-start | bytes 534536 | tf_op jit(solution)/shard_map/ppermute | solution.py:63
  16.3 14.3 %collective-permute-start.1 = (bf16[24,3712]{1,0:T(8,128)(2,1)S(1)}, bf16[24,3712]{1,0:T(8,128)(2,1)S(1)}, u32[]{:S(2)}, u32[]{:S(2)}) collective-permute-start(bf16[24,3712]{1,0:T(8,128)(2,1)S(1)} %get-tuple-element.14), channel_id=1, source_target_pairs={{8,0},{12,4},{0,8},{4,12},{9,1},{13,5},{1,9},{5,13},{10,2},{14,6},... | collective-permute-start | bytes 534536 | tf_op jit(solution)/shard_map/ppermute | solution.py:63
  16.3 14.3 %collective-permute-start.2 = (bf16[24,3712]{1,0:T(8,128)(2,1)S(1)}, bf16[24,3712]{1,0:T(8,128)(2,1)S(1)}, u32[]{:S(2)}, u32[]{:S(2)}) collective-permute-start(bf16[24,3712]{1,0:T(8,128)(2,1)S(1)} %get-tuple-element.14), channel_id=1, source_target_pairs={{12,0},{0,4},{4,8},{8,12},{13,1},{1,5},{5,9},{9,13},{14,2},{2,6},{... | collective-permute-start | bytes 534536 | tf_op jit(solution)/shard_map/ppermute | solution.py:63
  30.7 10.7 %collective-permute-start.3 = (bf16[96,3712]{1,0:T(8,128)(2,1)S(1)}, bf16[96,3712]{1,0:T(8,128)(2,1)S(1)}, u32[]{:S(2)}, u32[]{:S(2)}) collective-permute-start(bf16[96,3712]{1,0:T(8,128)(2,1)S(1)} %pad_maximum_fusion.1), channel_id=1, source_target_pairs={{64,0},{128,64},{192,128},{0,192},{66,2},{130,66},{194,130},{2,194... | collective-permute-start | bytes 2138120 | tf_op jit(solution)/shard_map/ppermute | solution.py:26
  41.4 1.1 copy-start
  42.6 96.6 %all-gather.5.cloned.1.call-start = ((), (), s32[]{:S(2)}) async-start(), calls=%async_computation.4 | async-start | bytes 7127040 | tf_op jit(solution)/shard_map/all_gather | solution.py:70
  42.6 12.0 %collective-permute-start.4 = (bf16[96,3712]{1,0:T(8,128)(2,1)S(1)}, bf16[96,3712]{1,0:T(8,128)(2,1)S(1)}, u32[]{:S(2)}, u32[]{:S(2)}) collective-permute-start(bf16[96,3712]{1,0:T(8,128)(2,1)S(1)} %pad_maximum_fusion.1), channel_id=1, source_target_pairs={{128,0},{192,64},{0,128},{64,192},{130,2},{194,66},{2,130},{66,194... | collective-permute-start | bytes 2138120 | tf_op jit(solution)/shard_map/ppermute | solution.py:26
  45.2 17.0 %collective-permute-start.5 = (bf16[96,3712]{1,0:T(8,128)(2,1)S(1)}, bf16[96,3712]{1,0:T(8,128)(2,1)S(1)}, u32[]{:S(2)}, u32[]{:S(2)}) collective-permute-start(bf16[96,3712]{1,0:T(8,128)(2,1)S(1)} %pad_maximum_fusion.1), channel_id=1, source_target_pairs={{192,0},{0,64},{64,128},{128,192},{194,2},{2,66},{66,130},{130,194... | collective-permute-start | bytes 2138120 | tf_op jit(solution)/shard_map/ppermute | solution.py:26
  88.0 9.7 %collective-permute-start.6 = (bf16[768,3712]{1,0:T(8,128)(2,1)}, bf16[768,3712]{1,0:T(8,128)(2,1)}, u32[]{:S(2)}, u32[]{:S(2)}) collective-permute-start(bf16[768,3712]{1,0:T(8,128)(2,1)} %all-gather.3.cloned.1.call-done), channel_id=1, source_target_pairs={{0,1},{1,0},{2,3},{3,2},{4,5},{5,4},{6,7},{7,6},{8,9},{9,8},{10,11... | collective-permute-start | bytes 17104904 | tf_op jit(solution)/shard_map/ppermute | solution.py:74
  88.4 102.2 %reduce-scatter.3.cloned.1.call-start = ((), (), s32[]{:S(2)}) async-start(), calls=%async_computation.5 | async-start | bytes 6881280 | tf_op jit(solution)/shard_map/reduce_scatter | solution.py:82
  116.3 9.4 %collective-permute-start.7 = (bf16[768,3584]{1,0:T(8,128)(2,1)}, bf16[768,3584]{1,0:T(8,128)(2,1)}, u32[]{:S(2)}, u32[]{:S(2)}) collective-permute-start(bf16[768,3584]{1,0:T(8,128)(2,1)} %multiply_convert_fusion.1), channel_id=1, source_target_pairs={{0,1},{1,0},{2,3},{3,2},{4,5},{5,4},{6,7},{7,6},{8,9},{9,8},{10,11... | collective-permute-start | bytes 16515080 | tf_op jit(solution)/shard_map/ppermute | solution.py:77
  139.1 9.7 %collective-permute-start.9 = (bf16[768,3712]{1,0:T(8,128)(2,1)}, bf16[768,3712]{1,0:T(8,128)(2,1)}, u32[]{:S(2)}, u32[]{:S(2)}) collective-permute-start(bf16[768,3712]{1,0:T(8,128)(2,1)} %all-gather.5.cloned.1.call-done), channel_id=1, source_target_pairs={{0,1},{1,0},{2,3},{3,2},{4,5},{5,4},{6,7},{7,6},{8,9},{9,8},{10,11... | collective-permute-start | bytes 17104904 | tf_op jit(solution)/shard_map/ppermute | solution.py:74
  139.6 90.3 %reduce-scatter.5.cloned.1.call-start = ((), (), s32[]{:S(2)}) async-start(), calls=%async_computation.6 | async-start | bytes 6881280 | tf_op jit(solution)/shard_map/reduce_scatter | solution.py:82
  167.7 9.4 %collective-permute-start.10 = (bf16[768,3584]{1,0:T(8,128)(2,1)}, bf16[768,3584]{1,0:T(8,128)(2,1)}, u32[]{:S(2)}, u32[]{:S(2)}) collective-permute-start(bf16[768,3584]{1,0:T(8,128)(2,1)} %multiply_convert_fusion), channel_id=1, source_target_pairs={{0,1},{1,0},{2,3},{3,2},{4,5},{5,4},{6,7},{7,6},{8,9},{9,8},{10,11... | collective-permute-start | bytes 16515080 | tf_op jit(solution)/shard_map/ppermute | solution.py:77
  191.8 42.8 %collective-permute-start.8 = (bf16[96,3584]{1,0:T(8,128)(2,1)S(1)}, bf16[96,3584]{1,0:T(8,128)(2,1)S(1)}, u32[]{:S(2)}, u32[]{:S(2)}) collective-permute-start(bf16[96,3584]{1,0:T(8,128)(2,1)S(1)} %slice.131), channel_id=1, source_target_pairs={{0,64},{64,128},{128,192},{192,0},{2,66},{66,130},{130,194},{194,2... | collective-permute-start | bytes 2064392 | tf_op jit(solution)/shard_map/ppermute | solution.py:30
  231.2 11.7 %collective-permute-start.11 = (bf16[96,3584]{1,0:T(8,128)(2,1)S(1)}, bf16[96,3584]{1,0:T(8,128)(2,1)S(1)}, u32[]{:S(2)}, u32[]{:S(2)}) collective-permute-start(bf16[96,3584]{1,0:T(8,128)(2,1)S(1)} %get-tuple-element.17), channel_id=1, source_target_pairs={{0,128},{64,192},{128,0},{192,64},{2,130},{66,194},{130,2},{194,66... | collective-permute-start | bytes 2064392 | tf_op jit(solution)/shard_map/ppermute | solution.py:30
  233.7 16.4 %collective-permute-start.12 = (bf16[96,3584]{1,0:T(8,128)(2,1)S(1)}, bf16[96,3584]{1,0:T(8,128)(2,1)}, u32[]{:S(2)}, u32[]{:S(2)}) collective-permute-start(bf16[96,3584]{1,0:T(8,128)(2,1)S(1)} %get-tuple-element.18), channel_id=1, source_target_pairs={{0,192},{64,0},{128,64},{192,128},{2,194},{66,2},{130,66},{194,130... | collective-permute-start | bytes 2064392 | tf_op jit(solution)/shard_map/ppermute | solution.py:30
  251.9 11.5 %collective-permute-start.13 = (bf16[24,1792]{1,0:T(8,128)(2,1)S(1)}, bf16[24,1792]{1,0:T(8,128)(2,1)S(1)}, u32[]{:S(2)}, u32[]{:S(2)}) collective-permute-start(bf16[24,1792]{1,0:T(8,128)(2,1)S(1)} %get-tuple-element.19), channel_id=1, source_target_pairs={{0,2},{2,0},{4,6},{6,4},{8,10},{10,8},{12,14},{14,12},{1,3},{3,1},... | collective-permute-start | bytes 258056 | tf_op jit(solution)/shard_map/ppermute | solution.py:97
  257.4 9.8 %collective-permute-start.15 = (bf16[24,1792]{1,0:T(8,128)(2,1)S(1)}, bf16[24,1792]{1,0:T(8,128)(2,1)S(1)}, u32[]{:S(2)}, u32[]{:S(2)}) collective-permute-start(bf16[24,1792]{1,0:T(8,128)(2,1)S(1)} %get-tuple-element.22), channel_id=1, source_target_pairs={{0,6},{2,4},{4,10},{6,8},{8,14},{10,12},{12,2},{14,0},{1,7},{3,5},... | collective-permute-start | bytes 258056 | tf_op jit(solution)/shard_map/ppermute | solution.py:97
  257.5 13.2 %collective-permute-start.17 = (bf16[24,1792]{1,0:T(8,128)(2,1)S(1)}, bf16[24,1792]{1,0:T(8,128)(2,1)S(1)}, u32[]{:S(2)}, u32[]{:S(2)}) collective-permute-start(bf16[24,1792]{1,0:T(8,128)(2,1)S(1)} %get-tuple-element.21), channel_id=1, source_target_pairs={{0,10},{2,8},{4,14},{6,12},{8,2},{10,0},{12,6},{14,4},{1,11},{3,9}... | collective-permute-start | bytes 258056 | tf_op jit(solution)/shard_map/ppermute | solution.py:97
  260.4 12.2 %collective-permute-start.19 = (bf16[24,1792]{1,0:T(8,128)(2,1)S(1)}, bf16[24,1792]{1,0:T(8,128)(2,1)S(1)}, u32[]{:S(2)}, u32[]{:S(2)}) collective-permute-start(bf16[24,1792]{1,0:T(8,128)(2,1)S(1)} %get-tuple-element.20), channel_id=1, source_target_pairs={{0,14},{2,12},{4,2},{6,0},{8,6},{10,4},{12,10},{14,8},{1,15},{3,13... | collective-permute-start | bytes 258056 | tf_op jit(solution)/shard_map/ppermute | solution.py:97
  261.2 11.4 %collective-permute-start.14 = (bf16[24,1792]{1,0:T(8,128)(2,1)S(1)}, bf16[24,1792]{1,0:T(8,128)(2,1)S(1)}, u32[]{:S(2)}, u32[]{:S(2)}) collective-permute-start(bf16[24,1792]{1,0:T(8,128)(2,1)S(1)} %get-tuple-element.23), channel_id=1, source_target_pairs={{0,4},{2,6},{4,8},{6,10},{8,12},{10,14},{12,0},{14,2},{1,5},{3,7},... | collective-permute-start | bytes 258056 | tf_op jit(solution)/shard_map/ppermute | solution.py:97
  263.4 9.2 %collective-permute-start.16 = (bf16[24,1792]{1,0:T(8,128)(2,1)S(1)}, bf16[24,1792]{1,0:T(8,128)(2,1)S(1)}, u32[]{:S(2)}, u32[]{:S(2)}) collective-permute-start(bf16[24,1792]{1,0:T(8,128)(2,1)S(1)} %get-tuple-element.25), channel_id=1, source_target_pairs={{0,8},{2,10},{4,12},{6,14},{8,0},{10,2},{12,4},{14,6},{1,9},{3,11}... | collective-permute-start | bytes 258056 | tf_op jit(solution)/shard_map/ppermute | solution.py:97
  267.2 7.8 %collective-permute-start.18 = (bf16[24,1792]{1,0:T(8,128)(2,1)S(1)}, bf16[24,1792]{1,0:T(8,128)(2,1)S(1)}, u32[]{:S(2)}, u32[]{:S(2)}) collective-permute-start(bf16[24,1792]{1,0:T(8,128)(2,1)S(1)} %get-tuple-element.24), channel_id=1, source_target_pairs={{0,12},{2,14},{4,0},{6,2},{8,4},{10,6},{12,8},{14,10},{1,13},{3,15... | collective-permute-start | bytes 258056 | tf_op jit(solution)/shard_map/ppermute | solution.py:97
Sparse Core Ops, SparseCore 0:
  42.7 45.2 all-gather.2
  89.8 41.5 all-gather.4
  139.7 39.0 reduce-scatter.2
  190.7 39.0 reduce-scatter.4
